TPU v7x, 256 devices: a whole 4x4x8 slice. The times are simulated.
256 devices in a mesh: rows: 32 (over y, z), cols: 8 (over x, core).
Axes of the slice: x: 4, y: 4, z: 8, core: 2. Of those that a mesh axis runs over, the one named last changes fastest.
Arguments:
- snapshots: bfloat16 [524288, 2048], P(('rows', 'cols')), may hold values from -24 to 24
- test_matrix: bfloat16 [2048, 256], replicated, may hold values from -0.125 to 0.125
Outputs:
- basis: float32 [524288, 256], P(('rows', 'cols'))
- coeffs: float32 [256, 2048], P('rows', 'cols')
All inputs are finite; a program needn't handle non-finite values.
Results may differ from a plain program's by a relative error of at most 0.0005.
Values sent between devices are 32-bit elements; how exact they have to be, the bound alone decides.
A program may use at most 64 MiB of HBM per device.

v0:
```python
import math

import jax
import jax.numpy as jnp
from jax import lax
from jax.sharding import PartitionSpec as P


def cross_product(left, right):
    return lax.dot_general(
        left,
        right,
        (((0,), (0,)), ((), ())),
        precision=lax.Precision.HIGHEST,
        preferred_element_type=jnp.float32,
    )


def lower_inverse(gram):
    lower = jnp.linalg.cholesky(gram)
    identity = jnp.eye(gram.shape[0], dtype=gram.dtype)
    return jax.scipy.linalg.solve_triangular(lower, identity, lower=True)


def body(snapshots, test_matrix):
    n_rows = lax.axis_size("rows")
    n_cols = lax.axis_size("cols")
    rows_here = snapshots.shape[0]
    total_rows = rows_here * n_rows * n_cols
    sketch = jnp.dot(snapshots, test_matrix, preferred_element_type=jnp.float32)
    gram_local = cross_product(sketch, sketch)
    summed = lax.psum(gram_local, ("rows", "cols"))
    inverse_low = lower_inverse(summed)
    basis_full = lax.dot_general(
        sketch,
        inverse_low,
        (((1,), (1,)), ((), ())),
        precision=lax.Precision.HIGHEST,
        preferred_element_type=jnp.float32,
    ) * math.sqrt(total_rows)
    basis_half = basis_full.astype(jnp.bfloat16)
    grid_part = lax.psum_scatter(
        lax.dot_general(
            snapshots, basis_half, (((0,), (0,)), ((), ())), preferred_element_type=jnp.float32
        ),
        "cols",
        scatter_dimension=0,
        tiled=True,
    )
    projected = lax.psum_scatter(grid_part.T, "rows", scatter_dimension=0, tiled=True)
    coeffs = projected * (1.0 / math.sqrt(total_rows))
    return (basis_full, coeffs)


def solution(mesh):
    placed = (P(("rows", "cols"), None), P())
    return jax.shard_map(
        body,
        mesh=mesh,
        in_specs=placed,
        out_specs=(P(("rows", "cols"), None), P("rows", "cols")),
        check_vma=False,
    )
```

profile of v0, /device:TPU:1, one launch (start us, length us, event | category | flops | bytes accessed | tf_op | source)
XLA Modules:
  0.0 610.0 jit_solution(18201936936618423826)
XLA Ops:
  7.2 0.0 copy-start
  7.2 0.0 all-reduce.3.cloned.1.call-start
  7.2 1.2 copy-done
  8.4 5.7 fusion.14
  14.1 4.2 fusion.15
  18.3 0.0 all-reduce.3.cloned.1.call-update
  18.3 0.2 reduce-scatter.3.cloned.1.call-start
  18.6 252.5 %all-reduce.3.cloned.1.call-done = f32[256,256]{0,1:T(8,128)} async-done(((f32[256,256]{0,1:T(8,128)}), f32[256,256]{0,1:T(8,128)}) %all-reduce.3.cloned.1.call-update) | async-done | bytes 262160 | tf_op jit(solution)/shard_map/psum | solution.py:32
  271.1 1.1 copy.5
  272.2 1.0 fusion.4
  273.2 0.0 copy-start.3
  273.2 0.7 copy-done.3
  273.9 11.7 %cholesky.50 = f32[128,128]{1,0:T(8,128)S(1)} custom-call(f32[128,128]{1,0:T(8,128)S(1)} %cholesky.118), custom_call_target="Cholesky" | custom-call | tf_op jit(solution)/shard_map/jit(cholesky)/cholesky | solution.py:20
  285.6 10.4 %custom-call.15 = f32[1,128,128]{1,2,0:T(8,128)} custom-call(f32[1,128,128]{2,1,0:T(8,128)S(1)} %get-tuple-element.23), custom_call_target="InvertDiagBlocksLowerTriangular" | custom-call | tf_op jit(solution)/shard_map/jit(cholesky)/cholesky | solution.py:20
  296.1 1.1 constant_dynamic-update-slice_fusion.1
  297.2 1.7 convolution_subtract_fusion.1
  298.9 12.5 %cholesky.105 = f32[128,128]{1,0:T(8,128)S(1)} custom-call(f32[128,128]{1,0:T(8,128)} %convolution_subtract_fusion.1), custom_call_target="Cholesky" | custom-call | tf_op jit(solution)/shard_map/jit(cholesky)/cholesky | solution.py:20
  311.5 0.0 copy-start.2
  311.5 0.7 compare_reduce_fusion
  313.5 0.0 copy-done.2
  313.5 1.0 select_select_fusion
  314.5 0.1 triangular_solve.63
  314.6 5.5 while.1
  314.7 0.6 fusion.27
  315.3 2.0 bitcast_dynamic-update-slice_fusion.2
  317.4 0.6 fusion.27
  318.0 2.1 bitcast_dynamic-update-slice_fusion.2
  320.0 21.1 %custom-call.16 = f32[2,128,128]{1,2,0:T(8,128)} custom-call(f32[2,128,128]{2,1,0:T(8,128)} %get-tuple-element.9), custom_call_target="InvertDiagBlocksLowerTriangular" | custom-call | tf_op jit(solution)/shard_map/jit(_solve_triangular)/triangular_solve | solution.py:22
  341.2 1.1 fusion.5
  342.3 0.3 convolution_subtract_fusion
  342.5 1.2 fusion.8
  343.7 1.9 convolution_multiply_fusion
  345.6 0.0 copy-start.1
  345.6 1.3 copy-done.1
  347.0 7.1 %convolution_bitcast_fusion = f32[2048,256]{0,1:T(8,128)} fusion(bf16[2048,2048]{1,0:T(8,128)(2,1)} %param.2, f32[2048,256]{1,0:T(8,128)S(1)} %convolution_multiply_fusion), kind=kOutput, calls=%fused_computation.2 | convolution fusion | flops 2148007936 | bytes 12582912 | tf_op jit(solution)/shard_map/dot_general | solution.py:43
  354.1 0.0 reduce-scatter.3.cloned.1.call-update
  354.1 0.0 reduce-scatter.5.cloned.1.call-start
  354.2 33.8 %reduce-scatter.3.cloned.1.call-done = f32[256,256]{0,1:T(8,128)} async-done(((f32[2048,256]{0,1:T(8,128)}), f32[256,256]{0,1:T(8,128)}) %reduce-scatter.3.cloned.1.call-update) | async-done | bytes 262160 | tf_op jit(solution)/shard_map/reduce_scatter | solution.py:42
  388.0 0.0 reduce-scatter.5.cloned.1.call-update
  388.0 214.1 %reduce-scatter.5.cloned.1.call-done = f32[8,256]{1,0:T(8,128)} async-done(((f32[256,256]{1,0:T(8,128)}), f32[8,256]{1,0:T(8,128)}) %reduce-scatter.5.cloned.1.call-update) | async-done | bytes 8208 | tf_op jit(solution)/shard_map/reduce_scatter | solution.py:50
  602.1 1.3 broadcast_multiply_fusion
  (9 shorter events, 0.1 us)
Async XLA Ops:
  7.2 1.2 copy-start
  7.2 263.9 %all-reduce.3.cloned.1.call-start = ((), (), s32[]{:S(2)}) async-start(), calls=%async_computation.2 | async-start | bytes 524288 | tf_op jit(solution)/shard_map/psum | solution.py:32
  18.3 369.7 %reduce-scatter.3.cloned.1.call-start = ((), (), s32[]{:S(2)}) async-start(), calls=%async_computation.3 | async-start | bytes 2359296 | tf_op jit(solution)/shard_map/reduce_scatter | solution.py:42
  273.2 0.7 copy-start.3
  311.5 2.0 copy-start.2
  345.6 1.3 copy-start.1
  354.1 248.0 %reduce-scatter.5.cloned.1.call-start = ((), (), s32[]{:S(2)}) async-start(), calls=%async_computation.4 | async-start | bytes 270336 | tf_op jit(solution)/shard_map/reduce_scatter | solution.py:50
Sparse Core Ops, SparseCore 0:
  18.4 252.6 all-reduce.2
  354.2 33.6 reduce-scatter.2
  391.8 210.2 reduce-scatter.4
where the time goes:
time: 615 us; the launch traced here: 610 us
  waiting for transfers between devices  500 us (81%)
  other arithmetic  59.9 us (10%)
  matrix products  24.3 us (4%)
  between operations  15.1 us (2%)
  local copies, waits for them, and re-layouts  9.67 us (2%)
    psum x1, waiting for transfers between devices, body(): summed = lax.psum(gram_local, ('rows', 'cols'))  253 us
    reduce_scatter x1, waiting for transfers between devices, body(): lax.psum_scatter(grid_part.T, 'rows', scatter_dimension=0, tiled=True)  214 us
    another operation x6, other arithmetic, lower_inverse(): lower = jnp.linalg.cholesky(gram)  35.5 us
    reduce_scatter x1, waiting for transfers between devices, body(): lax.psum_scatter(lax.dot_general(snapshots, basis_half, (((0,), (0,)), ((...  33.8 us
    another operation x3, other arithmetic, lower_inverse(): return jax.scipy.linalg.solve_triangular(lower, identity, lower=True)  22.1 us
  transfers between devices with their start and end apart: 3, of which 3 were waited for; matrix products, arithmetic and copies ran while one was open for 0% of the time, Pallas kernels for 0%

commit v1 on v0

--- a/solution.py
+++ b/solution.py
@@ -22,6 +22,19 @@
     return jax.scipy.linalg.solve_triangular(lower, identity, lower=True)
 
 
+def reduce_scatter(x, axis, n):
+    chunks = x.reshape(n, x.shape[0] // n, *x.shape[1:])
+    return lax.all_to_all(chunks, axis, 0, 0, tiled=True).sum(0)
+
+
+def all_reduce(x):
+    axes = ("rows", "cols")
+    n = lax.axis_size(axes)
+    mine = reduce_scatter(x, axes, n)
+    spread = jnp.broadcast_to(mine[None], (n, *mine.shape))
+    return lax.all_to_all(spread, axes, 0, 0, tiled=True).reshape(x.shape)
+
+
 def body(snapshots, test_matrix):
     n_rows = lax.axis_size("rows")
     n_cols = lax.axis_size("cols")
@@ -29,7 +42,7 @@
     total_rows = rows_here * n_rows * n_cols
     sketch = jnp.dot(snapshots, test_matrix, preferred_element_type=jnp.float32)
     gram_local = cross_product(sketch, sketch)
-    summed = lax.psum(gram_local, ("rows", "cols"))
+    summed = all_reduce(gram_local)
     inverse_low = lower_inverse(summed)
     basis_full = lax.dot_general(
         sketch,
@@ -39,15 +52,11 @@
         preferred_element_type=jnp.float32,
     ) * math.sqrt(total_rows)
     basis_half = basis_full.astype(jnp.bfloat16)
-    grid_part = lax.psum_scatter(
-        lax.dot_general(
-            snapshots, basis_half, (((0,), (0,)), ((), ())), preferred_element_type=jnp.float32
-        ),
-        "cols",
-        scatter_dimension=0,
-        tiled=True,
+    partial = lax.dot_general(
+        snapshots, basis_half, (((0,), (0,)), ((), ())), preferred_element_type=jnp.float32
     )
-    projected = lax.psum_scatter(grid_part.T, "rows", scatter_dimension=0, tiled=True)
+    grid_part = reduce_scatter(partial, "cols", n_cols)
+    projected = reduce_scatter(grid_part.T, "rows", n_rows)
     coeffs = projected * (1.0 / math.sqrt(total_rows))
     return (basis_full, coeffs)
 

time: 615 us -> 191 us (0.31)
  waiting for transfers between devices: 500 us -> 15.2 us
  blocking collectives: 0 us -> 73.4 us
  between operations: 15.1 us -> 2.06 us
    psum x1 -> x0, waiting for transfers between devices: 253 us -> none  [body(): summed = lax.psum(gram_local, ('rows', 'cols'))]
    reduce_scatter x2 -> x0, waiting for transfers between devices: 248 us -> none  [the longest x1 214 us: body(): lax.psum_scatter(grid_part.T, 'rows', scatter_dimension=0, tiled=True)]
    all_to_all x0 -> x3, blocking collectives: none -> 73.4 us  [reduce_scatter(): return lax.all_to_all(chunks, axis, 0, 0, tiled=True).sum(0)]
    all_to_all x0 -> x1, waiting for transfers between devices: none -> 15.2 us  [all_reduce(): return lax.all_to_all(spread, axes, 0, 0, tiled=True).reshape(x.shape)]
  transfers between devices with their start and end apart: 3 -> 1, of which waited for: 3 -> 1; matrix products, arithmetic and copies ran while one was open for 0% -> 0% of each run, Pallas kernels for 0% -> 0%
where the time goes in v1:
time: 191 us; the launch traced here: 189 us
  blocking collectives  73.4 us (38%)
  other arithmetic  60.5 us (32%)
  matrix products  23 us (12%)
  waiting for transfers between devices  15.2 us (8%)
  local copies, waits for them, and re-layouts  9.17 us (5%)
  starting transfers between devices  5.35 us (3%)
  between operations  2.06 us (1%)
    all_to_all x3, blocking collectives, reduce_scatter(): return lax.all_to_all(chunks, axis, 0, 0, tiled=True).sum(0)  73.4 us
    another operation x6, other arithmetic, lower_inverse(): lower = jnp.linalg.cholesky(gram)  36.3 us
    another operation x3, other arithmetic, lower_inverse(): return jax.scipy.linalg.solve_triangular(lower, identity, lower=True)  22.1 us
    all_to_all x1, waiting for transfers between devices, all_reduce(): return lax.all_to_all(spread, axes, 0, 0, tiled=True).reshape(x.shape)  15.2 us
    dot_general x1, matrix products, body(): lax.dot_general(snapshots, basis_half, (((0,), (0,)), ((), ())), preferre...  6.55 us
    dot_general x1, matrix products, body(): sketch = jnp.dot(snapshots, test_matrix, preferred_element_type=jnp.float32)  5.73 us
    all_to_all x1, starting transfers between devices, all_reduce(): return lax.all_to_all(spread, axes, 0, 0, tiled=True).reshape(x.shape)  5.35 us
    another operation x6, local copies, waits for them, and re-layouts  5.02 us
  transfers between devices with their start and end apart: 1, of which 1 were waited for; matrix products, arithmetic and copies ran while one was open for 0% of the time, Pallas kernels for 0%

profile of v1, /device:TPU:1, one launch (start us, length us, event | category | flops | bytes accessed | tf_op | source)
XLA Modules:
  0.0 188.7 jit_solution(492838582462829359)
XLA Ops:
  0.6 0.0 copy-start
  0.6 1.2 copy-done
  1.9 5.7 %fusion.15 = f32[2048,256]{1,0:T(8,128)S(1)} fusion(bf16[2048,2048]{1,0:T(8,128)(2,1)} %param.2, bf16[2048,256]{1,0:T(8,128)(2,1)S(1)} %copy-done), kind=kOutput, calls=%fused_computation.39 | convolution fusion | flops 2147483648 | bytes 11534336 | tf_op jit(solution)/shard_map/dot_general | solution.py:43
  7.6 3.5 %convolution_bitcast_fusion = f32[256,1,256]{2,0,1:T(8,128)S(1)} fusion(f32[2048,256]{1,0:T(8,128)S(1)} %fusion.15), kind=kOutput, calls=%fused_computation.4 | convolution fusion | flops 1610612736 | bytes 2359296 | tf_op jit(solution)/shard_map/dot_general | solution.py:10
  11.1 0.3 copy.6
  11.4 31.0 %all_to_all.20 = f32[256,1,256]{2,1,0:T(1,128)S(1)} all-to-all(f32[256,1,256]{2,1,0:T(1,128)S(1)} %copy.6), channel_id=1, replica_groups=mesh['rows'=32,'cols'=8] {'rows','cols'}, dimensions={0} | all-to-all | bytes 524288 | tf_op jit(solution)/shard_map/all_to_all | solution.py:27
  42.3 0.3 reduce_sum.27
  42.6 0.8 broadcast_in_dim.3
  43.5 5.3 %all-to-all-start.1 = ((f32[256,1,256]{2,1,0:T(1,128)}), f32[256,1,256]{2,1,0:T(1,128)S(1)}, u32[]{:S(2)}, u32[]{:S(2)}) async-start(f32[256,1,256]{2,1,0:T(1,128)} %broadcast_in_dim.3), calls=%async_computation.1 | async-start | bytes 524288 | tf_op jit(solution)/shard_map/all_to_all | solution.py:35
  48.9 15.2 %all-to-all-done.1 = f32[256,1,256]{2,1,0:T(1,128)S(1)} async-done(((f32[256,1,256]{2,1,0:T(1,128)}), f32[256,1,256]{2,1,0:T(1,128)S(1)}, u32[]{:S(2)}, u32[]{:S(2)}) %all-to-all-start.1) | async-done | bytes 262176 | tf_op jit(solution)/shard_map/all_to_all | solution.py:35
  64.1 0.8 copy.7
  65.0 1.0 fusion.5
  65.9 0.0 copy-start.3
  66.0 0.7 copy-done.3
  66.7 11.7 %cholesky.50 = f32[128,128]{1,0:T(8,128)S(1)} custom-call(f32[128,128]{1,0:T(8,128)S(1)} %cholesky.118), custom_call_target="Cholesky" | custom-call | tf_op jit(solution)/shard_map/jit(cholesky)/cholesky | solution.py:20
  78.4 0.6 select_reduce_fusion.1
  79.0 10.6 %custom-call.15 = f32[1,128,128]{1,2,0:T(8,128)S(1)} custom-call(f32[1,128,128]{2,1,0:T(8,128)} %get-tuple-element.23), custom_call_target="InvertDiagBlocksLowerTriangular" | custom-call | tf_op jit(solution)/shard_map/jit(cholesky)/cholesky | solution.py:20
  89.7 1.0 constant_dynamic-update-slice_fusion.1
  90.7 1.7 convolution_subtract_fusion.1
  92.5 12.5 %cholesky.105 = f32[128,128]{1,0:T(8,128)S(1)} custom-call(f32[128,128]{1,0:T(8,128)} %convolution_subtract_fusion.1), custom_call_target="Cholesky" | custom-call | tf_op jit(solution)/shard_map/jit(cholesky)/cholesky | solution.py:20
  105.1 0.0 copy-start.2
  105.1 0.7 compare_reduce_fusion
  107.0 0.0 copy-done.2
  107.0 1.0 select_select_fusion
  108.0 0.1 triangular_solve.63
  108.1 5.0 %while.1 = (s32[]{:T(128)}, f32[256,256]{1,0:T(8,128)S(1)}, s32[2,2]{1,0:T(2,128)S(1)}, f32[2,128,128]{2,1,0:T(8,128)}, s32[]{:T(128)}) while((s32[]{:T(128)}, f32[256,256]{1,0:T(8,128)S(1)}, s32[2,2]{1,0:T(2,128)S(1)}, f32[2,128,128]{2,1,0:T(8,128)}, s32[]{:T(128)}) %tuple.27), condition=%wide.while_cond, body=%wide.while_body.sunk | while | flops 2 | bytes 132205 | solution.py:22
  108.1 0.6 fusion.27
  108.7 1.9 %bitcast_dynamic-update-slice_fusion.2 = f32[2,128,128]{2,1,0:T(8,128)} fusion(f32[2,128,128]{2,1,0:T(8,128)} %get-tuple-element.65, s32[]{:T(128)S(6)} %copy.20, f32[256,256]{1,0:T(8,128)S(1)} %get-tuple-element.68, s32[]{:T(128)} %bitcast.49, s32[]{:T(128)} %bitcast.50), kind=kLoop, calls=%fused_computation.clone.1 | loop fusion | bytes 132100 | tf_op jit(solution)/shard_map/jit(_solve_triangular)/triangular_solve
  110.6 0.6 fusion.27
  111.2 1.9 %bitcast_dynamic-update-slice_fusion.2 = f32[2,128,128]{2,1,0:T(8,128)} fusion(f32[2,128,128]{2,1,0:T(8,128)} %get-tuple-element.65, s32[]{:T(128)S(6)} %copy.20, f32[256,256]{1,0:T(8,128)S(1)} %get-tuple-element.68, s32[]{:T(128)} %bitcast.49, s32[]{:T(128)} %bitcast.50), kind=kLoop, calls=%fused_computation.clone.1 | loop fusion | bytes 132100 | tf_op jit(solution)/shard_map/jit(_solve_triangular)/triangular_solve
  113.1 21.1 %custom-call.16 = f32[2,128,128]{1,2,0:T(8,128)} custom-call(f32[2,128,128]{2,1,0:T(8,128)} %get-tuple-element.9), custom_call_target="InvertDiagBlocksLowerTriangular" | custom-call | tf_op jit(solution)/shard_map/jit(_solve_triangular)/triangular_solve | solution.py:22
  134.2 1.1 fusion.6
  135.3 0.3 convolution_subtract_fusion
  135.6 1.2 fusion.9
  136.8 1.9 %convolution_multiply_fusion = f32[2048,256]{1,0:T(8,128)S(1)} fusion(f32[2048,256]{1,0:T(8,128)S(1)} %fusion.15, f32[128,256]{1,0:T(8,128)S(1)} %fusion.9, f32[128,256]{1,0:T(8,128)S(1)} %fusion.6), kind=kOutput, calls=%fused_computation.2 | convolution fusion | flops 1611202560 | bytes 4456448 | tf_op jit(solution)/shard_map/dot_general | solution.py:47
  138.7 0.0 copy-start.1
  138.7 6.5 %fusion = f32[256,2048]{1,0:T(8,128)S(1)} fusion(bf16[2048,2048]{1,0:T(8,128)(2,1)} %param.2, f32[2048,256]{1,0:T(8,128)S(1)} %convolution_multiply_fusion), kind=kOutput, calls=%fused_computation.7 | convolution fusion | flops 2148007936 | bytes 12582912 | tf_op jit(solution)/shard_map/dot_general | solution.py:55
  145.3 0.0 copy-done.1
  145.3 0.2 copy.14
  145.4 29.7 %all_to_all.21 = f32[8,256,256]{1,2,0:T(8,128)S(1)} all-to-all(f32[8,256,256]{1,2,0:T(8,128)S(1)} %bitcast.52), channel_id=1, replica_groups=mesh['rows'=32,'cols'=8] {'cols'}, dimensions={0} | all-to-all | bytes 4194304 | tf_op jit(solution)/shard_map/all_to_all | solution.py:27
  175.1 0.1 reduce_sum.28
  175.3 12.8 %all_to_all.22 = f32[32,8,256]{2,1,0:T(8,128)S(1)} all-to-all(f32[32,8,256]{2,1,0:T(8,128)S(1)} %bitcast.53), channel_id=1, replica_groups=mesh['rows'=32,'cols'=8] {'rows'}, dimensions={0} | all-to-all | bytes 524288 | tf_op jit(solution)/shard_map/all_to_all | solution.py:27
  188.1 0.6 broadcast_multiply_fusion
  (9 shorter events, 0.1 us)
Async XLA Ops:
  0.6 1.2 copy-start
  43.5 20.7 %all-to-all-start.1 = ((f32[256,1,256]{2,1,0:T(1,128)}), f32[256,1,256]{2,1,0:T(1,128)S(1)}, u32[]{:S(2)}, u32[]{:S(2)}) async-start(f32[256,1,256]{2,1,0:T(1,128)} %broadcast_in_dim.3), calls=%async_computation.1 | async-start | bytes 524288 | tf_op jit(solution)/shard_map/all_to_all | solution.py:35
  65.9 0.7 copy-start.3
  105.1 2.0 %copy-start.2 = (f32[256,256]{1,0:T(8,128)}, f32[256,256]{1,0:T(8,128)S(1)}, u32[]{:S(2)}) copy-start(f32[256,256]{1,0:T(8,128)S(1)} %get-tuple-element.21) | copy-start | bytes 786436
  138.7 6.6 %copy-start.1 = (f32[2048,256]{1,0:T(8,128)}, f32[2048,256]{1,0:T(8,128)S(1)}, u32[]{:S(2)}) copy-start(f32[2048,256]{1,0:T(8,128)S(1)} %convolution_multiply_fusion) | copy-start | bytes 6291460

commit v2 on v1

--- a/solution.py
+++ b/solution.py
@@ -16,10 +16,21 @@
     )
 
 
+def matmul(left, right):
+    return jnp.dot(left, right, precision=lax.Precision.HIGHEST, preferred_element_type=jnp.float32)
+
+
 def lower_inverse(gram):
-    lower = jnp.linalg.cholesky(gram)
-    identity = jnp.eye(gram.shape[0], dtype=gram.dtype)
-    return jax.scipy.linalg.solve_triangular(lower, identity, lower=True)
+    half = gram.shape[0] // 2
+    identity = jnp.eye(half, dtype=gram.dtype)
+    low11 = jnp.linalg.cholesky(gram[:half, :half])
+    inv11 = lax.linalg.triangular_solve(low11, identity, left_side=True, lower=True)
+    low21 = matmul(gram[half:, :half], inv11.T)
+    low22 = jnp.linalg.cholesky(gram[half:, half:] - matmul(low21, low21.T))
+    inv22 = lax.linalg.triangular_solve(low22, identity, left_side=True, lower=True)
+    inv21 = -matmul(inv22, matmul(low21, inv11))
+    top = jnp.concatenate([inv11, jnp.zeros_like(inv11)], axis=1)
+    return jnp.concatenate([top, jnp.concatenate([inv21, inv22], axis=1)], axis=0)
 
 
 def reduce_scatter(x, axis, n):

time: 191 us -> 168 us (0.88)
  blocking collectives: 73.4 us -> 94.4 us
  waiting for transfers between devices: 15.2 us -> 0 us
  other arithmetic: 60.5 us -> 47.6 us
  local copies, waits for them, and re-layouts: 9.17 us -> 3.18 us
  starting transfers between devices: 5.35 us -> 0 us
  matrix products: 23 us -> 20.1 us
    all_to_all x0 -> x1, blocking collectives: none -> 20.9 us  [all_reduce(): return lax.all_to_all(spread, axes, 0, 0, tiled=True).reshape(x.shape)]
    all_to_all x1 -> x0, waiting for transfers between devices: 15.2 us -> none  [all_reduce(): return lax.all_to_all(spread, axes, 0, 0, tiled=True).reshape(x.shape)]
    another operation x9 -> x10, other arithmetic: 58.4 us -> 46.5 us  [the longest x3 12.4 us: lower_inverse(): low22 = jnp.linalg.cholesky(gram[half:, half:] - matmul(low21, low21.T))]
    all_to_all x1 -> x0, starting transfers between devices: 5.35 us -> none  [all_reduce(): return lax.all_to_all(spread, axes, 0, 0, tiled=True).reshape(x.shape)]
    another operation x9 -> x1, local copies, waits for them, and re-layouts: 5.11 us -> 0.09 us  [lower_inverse(): lax.linalg.triangular_solve(low22, identity, left_side=True, lower=True)]
    another operation x5 -> x2, matrix products: 5.29 us -> 1.39 us  [the longest x1 1.12 us: lower_inverse(): lax.linalg.triangular_solve(low11, identity, left_side=True, lower=True)]
  transfers between devices with their start and end apart: 1 -> 0, of which waited for: 1 -> 0; matrix products, arithmetic and copies ran while one was open for 0% -> 0% of each run, Pallas kernels for 0% -> 0%
where the time goes in v2:
time: 168 us; the launch traced here: 166 us
  blocking collectives  94.4 us (56%)
  other arithmetic  47.6 us (28%)
  matrix products  20.1 us (12%)
  local copies, waits for them, and re-layouts  3.18 us (2%)
    all_to_all x3, blocking collectives, reduce_scatter(): return lax.all_to_all(chunks, axis, 0, 0, tiled=True).sum(0)  73.5 us
    all_to_all x1, blocking collectives, all_reduce(): return lax.all_to_all(spread, axes, 0, 0, tiled=True).reshape(x.shape)  20.9 us
    another operation x3, other arithmetic, lower_inverse(): low22 = jnp.linalg.cholesky(gram[half:, half:] - matmul(low21, low21.T))  12.4 us
    another operation x3, other arithmetic, lower_inverse(): low11 = jnp.linalg.cholesky(gram[:half, :half])  12.4 us
    another operation x2, other arithmetic, lower_inverse(): lax.linalg.triangular_solve(low11, identity, left_side=True, lower=True)  11.1 us
    another operation x2, other arithmetic, lower_inverse(): lax.linalg.triangular_solve(low22, identity, left_side=True, lower=True)  10.7 us
    dot_general x1, matrix products, body(): lax.dot_general(snapshots, basis_half, (((0,), (0,)), ((), ())), preferre...  6.55 us
    dot_general x1, matrix products, body(): sketch = jnp.dot(snapshots, test_matrix, preferred_element_type=jnp.float32)  5.73 us

profile of v2, /device:TPU:1, one launch (start us, length us, event | category | flops | bytes accessed | tf_op | source)
XLA Modules:
  0.0 166.1 jit_solution(14239216364780979679)
XLA Ops:
  0.6 0.0 copy-start
  0.6 1.2 copy-done
  1.9 5.7 %fusion.23 = f32[2048,256]{1,0:T(8,128)S(1)} fusion(bf16[2048,2048]{1,0:T(8,128)(2,1)} %param.5, bf16[2048,256]{1,0:T(8,128)(2,1)S(1)} %copy-done), kind=kOutput, calls=%fused_computation.41 | convolution fusion | flops 2147483648 | bytes 11534336 | tf_op jit(solution)/shard_map/dot_general | solution.py:54
  7.6 3.5 %convolution_bitcast_fusion = f32[256,1,256]{2,0,1:T(8,128)S(1)} fusion(f32[2048,256]{1,0:T(8,128)S(1)} %fusion.23), kind=kOutput, calls=%fused_computation.2 | convolution fusion | flops 1610612736 | bytes 2359296 | tf_op jit(solution)/shard_map/dot_general | solution.py:10
  11.1 0.3 copy.12
  11.4 31.0 %all_to_all.20 = f32[256,1,256]{2,1,0:T(1,128)S(1)} all-to-all(f32[256,1,256]{2,1,0:T(1,128)S(1)} %copy.12), channel_id=1, replica_groups=mesh['rows'=32,'cols'=8] {'rows','cols'}, dimensions={0} | all-to-all | bytes 524288 | tf_op jit(solution)/shard_map/all_to_all | solution.py:38
  42.3 0.3 reduce_sum.27
  42.6 0.1 broadcast_in_dim.2
  42.8 20.9 %all_to_all.21 = f32[256,1,256]{2,1,0:T(1,128)} all-to-all(f32[256,1,256]{2,1,0:T(1,128)S(1)} %broadcast_in_dim.2), channel_id=1, replica_groups=mesh['rows'=32,'cols'=8] {'rows','cols'}, dimensions={0} | all-to-all | bytes 524288 | tf_op jit(solution)/shard_map/all_to_all | solution.py:46
  63.7 1.1 copy.13
  64.8 0.1 copy.14
  64.9 11.7 %cholesky.44 = f32[128,128]{1,0:T(8,128)S(1)} custom-call(f32[128,128]{1,0:T(8,128)S(1)} %fusion.19), custom_call_target="Cholesky" | custom-call | tf_op jit(solution)/shard_map/jit(cholesky)/cholesky | solution.py:26
  76.6 0.6 compare_reduce_fusion.1
  77.3 0.7 fusion.12
  77.9 10.4 %custom-call.6 = f32[1,128,128]{1,2,0:T(8,128)} custom-call(f32[1,128,128]{2,1,0:T(8,128)S(1)} %fusion.12), custom_call_target="InvertDiagBlocksLowerTriangular" | custom-call | tf_op jit(solution)/shard_map/triangular_solve/custom-call.0 | solution.py:27
  88.4 1.1 fusion.10
  89.5 0.3 fusion.14
  89.8 0.3 convolution_subtract_fusion
  90.1 0.2 fusion.24
  90.3 0.1 copy.16
  90.4 11.7 %cholesky.55 = f32[128,128]{1,0:T(8,128)S(1)} custom-call(f32[128,128]{1,0:T(8,128)S(1)} %fusion.17), custom_call_target="Cholesky" | custom-call | tf_op jit(solution)/shard_map/jit(cholesky)/cholesky | solution.py:29
  102.1 0.6 compare_reduce_fusion
  102.8 0.7 fusion.13
  103.5 10.0 %custom-call.7 = f32[1,128,128]{1,2,0:T(8,128)S(1)} custom-call(f32[1,128,128]{2,1,0:T(8,128)S(1)} %fusion.13), custom_call_target="InvertDiagBlocksLowerTriangular" | custom-call | tf_op jit(solution)/shard_map/triangular_solve/custom-call.0 | solution.py:30
  113.4 0.3 fusion.8
  113.7 0.1 copy.18
  113.8 0.3 convolution_negate_fusion
  114.1 1.9 %convolution_multiply_fusion = f32[2048,256]{1,0:T(8,128)S(1)} fusion(f32[2048,256]{1,0:T(8,128)S(1)} %fusion.23, f32[128,128]{1,0:T(8,128)S(1)} %fusion.10, f32[128,128]{1,0:T(8,128)S(1)} %copy.18, f32[128,128]{1,0:T(8,128)S(1)} %convolution_negate_fusion), kind=kOutput, calls=%fused_computation | convolution fusion | flops 1611399168 | bytes 4390912 | tf_op jit(solution)/shard_map/dot_general | solution.py:58
  116.0 0.0 copy-start.1
  116.0 6.5 %fusion = f32[256,2048]{1,0:T(8,128)S(1)} fusion(bf16[2048,2048]{1,0:T(8,128)(2,1)} %param.5, f32[2048,256]{1,0:T(8,128)S(1)} %convolution_multiply_fusion), kind=kOutput, calls=%fused_computation.5 | convolution fusion | flops 2148007936 | bytes 12582912 | tf_op jit(solution)/shard_map/dot_general | solution.py:66
  122.6 0.0 copy-done.1
  122.6 0.2 copy.24
  122.8 29.7 %all_to_all.22 = f32[8,256,256]{1,2,0:T(8,128)S(1)} all-to-all(f32[8,256,256]{1,2,0:T(8,128)S(1)} %bitcast.43), channel_id=1, replica_groups=mesh['rows'=32,'cols'=8] {'cols'}, dimensions={0} | all-to-all | bytes 4194304 | tf_op jit(solution)/shard_map/all_to_all | solution.py:38
  152.5 0.1 reduce_sum.28
  152.6 12.8 %all_to_all.23 = f32[32,8,256]{2,1,0:T(8,128)S(1)} all-to-all(f32[32,8,256]{2,1,0:T(8,128)S(1)} %bitcast.44), channel_id=1, replica_groups=mesh['rows'=32,'cols'=8] {'rows'}, dimensions={0} | all-to-all | bytes 524288 | tf_op jit(solution)/shard_map/all_to_all | solution.py:38
  165.5 0.6 broadcast_multiply_fusion
  (6 shorter events, 0.1 us)
Async XLA Ops:
  0.6 1.2 copy-start
  116.0 6.6 %copy-start.1 = (f32[2048,256]{1,0:T(8,128)}, f32[2048,256]{1,0:T(8,128)S(1)}, u32[]{:S(2)}) copy-start(f32[2048,256]{1,0:T(8,128)S(1)} %convolution_multiply_fusion) | copy-start | bytes 6291460

commit v3 on v2

--- a/solution.py
+++ b/solution.py
@@ -1,8 +1,11 @@
+import functools
 import math
 
 import jax
 import jax.numpy as jnp
 from jax import lax
+from jax.experimental import pallas as pl
+from jax.experimental.pallas import tpu as pltpu
 from jax.sharding import PartitionSpec as P
 
 
@@ -38,12 +41,91 @@
     return lax.all_to_all(chunks, axis, 0, 0, tiled=True).sum(0)
 
 
+def all_reduce_kernel(n_cols, n, local_ref, out_ref, recv, mine, send1, recv1, send2, recv2):
+    me = lax.axis_index("rows") * n_cols + lax.axis_index("cols")
+
+    def device(p):
+        return (p // n_cols, p % n_cols)
+
+    def peers(step):
+        def visit(i, carry):
+            p = lax.rem(me + 1 + i, n)
+            step(p)
+            return carry
+
+        lax.fori_loop(0, n - 1, visit, 0)
+
+    barrier = pltpu.get_barrier_semaphore()
+
+    def greet(p):
+        pl.semaphore_signal(barrier, inc=1, device_id=device(p), device_id_type=pl.DeviceIdType.MESH)
+
+    peers(greet)
+    pl.semaphore_wait(barrier, n - 1)
+
+    def scatter_copy(p):
+        return pltpu.make_async_remote_copy(
+            src_ref=local_ref.at[p],
+            dst_ref=recv.at[me],
+            send_sem=send1.at[p],
+            recv_sem=recv1.at[me],
+            device_id=device(p),
+            device_id_type=pl.DeviceIdType.MESH,
+        )
+
+    def arrived(sem, buffer, p):
+        return pltpu.make_async_remote_copy(
+            src_ref=buffer.at[p],
+            dst_ref=buffer.at[p],
+            send_sem=sem.at[p],
+            recv_sem=sem.at[p],
+            device_id=device(p),
+            device_id_type=pl.DeviceIdType.MESH,
+        )
+
+    peers(lambda p: scatter_copy(p).start())
+    recv[me] = local_ref[me]
+    peers(lambda p: arrived(recv1, recv, p).wait_recv())
+    peers(lambda p: scatter_copy(p).wait_send())
+    mine[...] = jnp.sum(recv[...], axis=0)
+
+    def gather_copy(p):
+        return pltpu.make_async_remote_copy(
+            src_ref=mine,
+            dst_ref=out_ref.at[me],
+            send_sem=send2.at[p],
+            recv_sem=recv2.at[me],
+            device_id=device(p),
+            device_id_type=pl.DeviceIdType.MESH,
+        )
+
+    peers(lambda p: gather_copy(p).start())
+    out_ref[me] = mine[...]
+    peers(lambda p: arrived(recv2, out_ref, p).wait_recv())
+    peers(lambda p: gather_copy(p).wait_send())
+
+
 def all_reduce(x):
-    axes = ("rows", "cols")
-    n = lax.axis_size(axes)
-    mine = reduce_scatter(x, axes, n)
-    spread = jnp.broadcast_to(mine[None], (n, *mine.shape))
-    return lax.all_to_all(spread, axes, 0, 0, tiled=True).reshape(x.shape)
+    n_cols = lax.axis_size("cols")
+    n = lax.axis_size("rows") * n_cols
+    rows, width = x.shape
+    block = (n, rows // n, width)
+    out = pl.pallas_call(
+        functools.partial(all_reduce_kernel, n_cols, n),
+        out_shape=jax.ShapeDtypeStruct(block, x.dtype),
+        in_specs=[pl.BlockSpec(memory_space=pltpu.VMEM)],
+        out_specs=pl.BlockSpec(memory_space=pltpu.VMEM),
+        scratch_shapes=[
+            pltpu.VMEM(block, x.dtype),
+            pltpu.VMEM(block[1:], x.dtype),
+            pltpu.SemaphoreType.DMA((n,)),
+            pltpu.SemaphoreType.DMA((n,)),
+            pltpu.SemaphoreType.DMA((n,)),
+            pltpu.SemaphoreType.DMA((n,)),
+        ],
+        compiler_params=pltpu.CompilerParams(collective_id=0, has_side_effects=True),
+    )(x.reshape(block))
+    return out.reshape(rows, width)
 
 
 def body(snapshots, test_matrix):

time: 168 us -> 177 us (1.054)
  Pallas kernels: 0 us -> 57.5 us
  blocking collectives: 94.4 us -> 44.8 us
    pallas_call x0 -> x1, Pallas kernels: none -> 57.5 us  [all_reduce(): pl.pallas_call(functools.partial(all_reduce_kernel, n_cols, n), out_shape...]
    all_to_all x3 -> x2, blocking collectives: 73.5 us -> 44.8 us  [reduce_scatter(): return lax.all_to_all(chunks, axis, 0, 0, tiled=True).sum(0)]
    all_to_all x1 -> x0, blocking collectives: 20.9 us -> none  [all_reduce(): return lax.all_to_all(spread, axes, 0, 0, tiled=True).reshape(x.shape)]
where the time goes in v3:
time: 177 us; the launch traced here: 174 us
  Pallas kernels  57.5 us (32%)
  other arithmetic  47.3 us (27%)
  blocking collectives  44.8 us (25%)
  matrix products  20.1 us (11%)
  local copies, waits for them, and re-layouts  3.65 us (2%)
    pallas_call x1, Pallas kernels, all_reduce(): pl.pallas_call(functools.partial(all_reduce_kernel, n_cols, n), out_shape...  57.5 us
    all_to_all x2, blocking collectives, reduce_scatter(): return lax.all_to_all(chunks, axis, 0, 0, tiled=True).sum(0)  44.8 us
    another operation x3, other arithmetic, lower_inverse(): low22 = jnp.linalg.cholesky(gram[half:, half:] - matmul(low21, low21.T))  12.6 us
    another operation x3, other arithmetic, lower_inverse(): low11 = jnp.linalg.cholesky(gram[:half, :half])  12.4 us
    another operation x2, other arithmetic, lower_inverse(): lax.linalg.triangular_solve(low11, identity, left_side=True, lower=True)  11.1 us
    another operation x2, other arithmetic, lower_inverse(): lax.linalg.triangular_solve(low22, identity, left_side=True, lower=True)  10.5 us
    dot_general x1, matrix products, body(): lax.dot_general(snapshots, basis_half, (((0,), (0,)), ((), ())), preferre...  6.55 us
    dot_general x1, matrix products, body(): sketch = jnp.dot(snapshots, test_matrix, preferred_element_type=jnp.float32)  5.73 us

profile of v3, /device:TPU:1, one launch (start us, length us, event | category | flops | bytes accessed | tf_op | source)
XLA Modules:
  0.0 174.2 jit_solution(17865425943107614480)
XLA Ops:
  0.6 0.0 copy-start
  0.6 1.2 copy-done
  1.9 5.7 %fusion.23 = f32[2048,256]{1,0:T(8,128)S(1)} fusion(bf16[2048,2048]{1,0:T(8,128)(2,1)} %param.5, bf16[2048,256]{1,0:T(8,128)(2,1)S(1)} %copy-done), kind=kOutput, calls=%fused_computation.40 | convolution fusion | flops 2147483648 | bytes 11534336 | tf_op jit(solution)/shard_map/dot_general | solution.py:136
  7.6 3.5 %fusion.24 = f32[256,256]{1,0:T(8,128)S(1)} fusion(f32[2048,256]{1,0:T(8,128)S(1)} %fusion.23), kind=kOutput, calls=%fused_computation.41 | convolution fusion | flops 1610612736 | bytes 2359296 | tf_op jit(solution)/shard_map/dot_general | solution.py:13
  11.1 0.9 reshape.27.local_ref
  12.0 57.5 %shard_map.41 = f32[256,1,256]{2,1,0:T(1,128)} custom-call(f32[256,1,256]{2,1,0:T(1,128)} %reshape.27.local_ref), custom_call_target="tpu_custom_call" | custom-call | tf_op jit(solution)/shard_map/pallas_call | solution.py:113
  69.5 1.1 copy.14
  70.6 0.1 copy.15
  70.7 11.7 %cholesky.44 = f32[128,128]{1,0:T(8,128)S(1)} custom-call(f32[128,128]{1,0:T(8,128)S(1)} %fusion.19), custom_call_target="Cholesky" | custom-call | tf_op jit(solution)/shard_map/jit(cholesky)/cholesky | solution.py:29
  82.4 0.6 compare_reduce_fusion.1
  83.1 0.7 fusion.12
  83.7 10.4 %custom-call.6 = f32[1,128,128]{1,2,0:T(8,128)} custom-call(f32[1,128,128]{2,1,0:T(8,128)S(1)} %fusion.12), custom_call_target="InvertDiagBlocksLowerTriangular" | custom-call | tf_op jit(solution)/shard_map/triangular_solve/custom-call.0 | solution.py:30
  94.2 1.1 fusion.10
  95.3 0.3 fusion.14
  95.6 0.3 convolution_subtract_fusion
  95.9 0.2 fusion.25
  96.1 0.1 copy.17
  96.2 11.9 %cholesky.55 = f32[128,128]{1,0:T(8,128)S(1)} custom-call(f32[128,128]{1,0:T(8,128)S(1)} %fusion.17), custom_call_target="Cholesky" | custom-call | tf_op jit(solution)/shard_map/jit(cholesky)/cholesky | solution.py:32
  108.1 0.6 compare_reduce_fusion
  108.8 0.7 fusion.13
  109.4 9.8 %custom-call.7 = f32[1,128,128]{1,2,0:T(8,128)S(1)} custom-call(f32[1,128,128]{2,1,0:T(8,128)S(1)} %fusion.13), custom_call_target="InvertDiagBlocksLowerTriangular" | custom-call | tf_op jit(solution)/shard_map/triangular_solve/custom-call.0 | solution.py:33
  119.2 0.3 fusion.8
  119.5 0.1 copy.19
  119.6 0.3 convolution_negate_fusion
  119.9 1.9 %convolution_multiply_fusion = f32[2048,256]{1,0:T(8,128)S(1)} fusion(f32[2048,256]{1,0:T(8,128)S(1)} %fusion.23, f32[128,128]{1,0:T(8,128)S(1)} %fusion.10, f32[128,128]{1,0:T(8,128)S(1)} %copy.19, f32[128,128]{1,0:T(8,128)S(1)} %convolution_negate_fusion), kind=kOutput, calls=%fused_computation | convolution fusion | flops 1611399168 | bytes 4390912 | tf_op jit(solution)/shard_map/dot_general | solution.py:140
  121.8 0.0 copy-start.1
  121.8 6.5 %fusion = f32[256,2048]{1,0:T(8,128)S(1)} fusion(bf16[2048,2048]{1,0:T(8,128)(2,1)} %param.5, f32[2048,256]{1,0:T(8,128)S(1)} %convolution_multiply_fusion), kind=kOutput, calls=%fused_computation.4 | convolution fusion | flops 2148007936 | bytes 12582912 | tf_op jit(solution)/shard_map/dot_general | solution.py:148
  128.4 0.0 copy-done.1
  128.4 0.2 copy.25
  128.6 29.3 %all_to_all.10 = f32[8,256,256]{1,2,0:T(8,128)S(1)} all-to-all(f32[8,256,256]{1,2,0:T(8,128)S(1)} %bitcast.41), channel_id=1, replica_groups=mesh['rows'=32,'cols'=8] {'cols'}, dimensions={0} | all-to-all | bytes 4194304 | tf_op jit(solution)/shard_map/all_to_all | solution.py:41
  157.9 0.1 reduce_sum.18
  158.0 15.6 %all_to_all.11 = f32[32,8,256]{2,1,0:T(8,128)S(1)} all-to-all(f32[32,8,256]{2,1,0:T(8,128)S(1)} %bitcast.42), channel_id=1, replica_groups=mesh['rows'=32,'cols'=8] {'rows'}, dimensions={0} | all-to-all | bytes 524288 | tf_op jit(solution)/shard_map/all_to_all | solution.py:41
  173.6 0.6 broadcast_multiply_fusion
  (6 shorter events, 0.1 us)
Async XLA Ops:
  0.6 1.2 copy-start
  121.8 6.6 %copy-start.1 = (f32[2048,256]{1,0:T(8,128)}, f32[2048,256]{1,0:T(8,128)S(1)}, u32[]{:S(2)}) copy-start(f32[2048,256]{1,0:T(8,128)S(1)} %convolution_multiply_fusion) | copy-start | bytes 6291460

commit v4 on v2

--- a/solution.py
+++ b/solution.py
@@ -1,8 +1,11 @@
+import functools
 import math
 
 import jax
 import jax.numpy as jnp
 from jax import lax
+from jax.experimental import pallas as pl
+from jax.experimental.pallas import tpu as pltpu
 from jax.sharding import PartitionSpec as P
 
 
@@ -38,12 +41,95 @@
     return lax.all_to_all(chunks, axis, 0, 0, tiled=True).sum(0)
 
 
+def all_reduce_kernel(n_rows, n_cols, local_ref, out_ref, recv1, part, recv2, total,
+                      send1, arrive1, send2, arrive2, send3, arrive3, send4, arrive4):
+    me_r = lax.axis_index("rows")
+    me_c = lax.axis_index("cols")
+
+    def along(n, mine, step):
+        def visit(i, carry):
+            step(lax.rem(mine + 1 + i, n))
+            return carry
+
+        lax.fori_loop(0, n - 1, visit, 0)
+
+    def copy(src, dst, send, arrive, device):
+        return pltpu.make_async_remote_copy(
+            src_ref=src, dst_ref=dst, send_sem=send, recv_sem=arrive,
+            device_id=device, device_id_type=pl.DeviceIdType.MESH,
+        )
+
+    barrier = pltpu.get_barrier_semaphore()
+    along(n_cols, me_c, lambda c: pl.semaphore_signal(
+        barrier, inc=1, device_id=(me_r, c), device_id_type=pl.DeviceIdType.MESH))
+    along(n_rows, me_r, lambda r: pl.semaphore_signal(
+        barrier, inc=1, device_id=(r, me_c), device_id_type=pl.DeviceIdType.MESH))
+    pl.semaphore_wait(barrier, n_cols + n_rows - 2)
+
+    def scatter1(c):
+        return copy(local_ref.at[c], recv1.at[me_c], send1.at[c], arrive1.at[me_c], (me_r, c))
+
+    along(n_cols, me_c, lambda c: scatter1(c).start())
+    recv1[me_c] = local_ref[me_c]
+    along(n_cols, me_c, lambda c: copy(recv1.at[c], recv1.at[c], send1.at[c], arrive1.at[c], (me_r, c)).wait_recv())
+    along(n_cols, me_c, lambda c: scatter1(c).wait_send())
+    summed = jnp.sum(recv1[...], axis=0)
+    share = part.shape[1]
+    for r in range(n_rows):
+        part[r] = summed[r * share:(r + 1) * share]
+
+    def scatter2(r):
+        return copy(part.at[r], recv2.at[me_r], send2.at[r], arrive2.at[me_r], (r, me_c))
+
+    along(n_rows, me_r, lambda r: scatter2(r).start())
+    recv2[me_r] = part[me_r]
+    along(n_rows, me_r, lambda r: copy(recv2.at[r], recv2.at[r], send2.at[r], arrive2.at[r], (r, me_c)).wait_recv())
+    along(n_rows, me_r, lambda r: scatter2(r).wait_send())
+    total[...] = jnp.sum(recv2[...], axis=0)
+
+    def gather3(r):
+        return copy(total, out_ref.at[me_c, me_r], send3.at[r], arrive3.at[me_r], (r, me_c))
+
+    along(n_rows, me_r, lambda r: gather3(r).start())
+    out_ref[me_c, me_r] = total[...]
+    along(n_rows, me_r, lambda r: copy(out_ref.at[me_c, r], out_ref.at[me_c, r], send3.at[r], arrive3.at[r], (r, me_c)).wait_recv())
+    along(n_rows, me_r, lambda r: gather3(r).wait_send())
+
+    def gather4(c):
+        return copy(out_ref.at[me_c], out_ref.at[me_c], send4.at[c], arrive4.at[me_c], (me_r, c))
+
+    along(n_cols, me_c, lambda c: gather4(c).start())
+    along(n_cols, me_c, lambda c: copy(out_ref.at[c], out_ref.at[c], send4.at[c], arrive4.at[c], (me_r, c)).wait_recv())
+    along(n_cols, me_c, lambda c: gather4(c).wait_send())
+
+
 def all_reduce(x):
-    axes = ("rows", "cols")
-    n = lax.axis_size(axes)
-    mine = reduce_scatter(x, axes, n)
-    spread = jnp.broadcast_to(mine[None], (n, *mine.shape))
-    return lax.all_to_all(spread, axes, 0, 0, tiled=True).reshape(x.shape)
+    n_rows = lax.axis_size("rows")
+    n_cols = lax.axis_size("cols")
+    rows, width = x.shape
+    block = rows // n_cols
+    out = pl.pallas_call(
+        functools.partial(all_reduce_kernel, n_rows, n_cols),
+        out_shape=jax.ShapeDtypeStruct((n_cols, n_rows, block // n_rows, width), x.dtype),
+        in_specs=[pl.BlockSpec(memory_space=pltpu.VMEM)],
+        out_specs=pl.BlockSpec(memory_space=pltpu.VMEM),
+        scratch_shapes=[
+            pltpu.VMEM((n_cols, block, width), x.dtype),
+            pltpu.VMEM((n_rows, block // n_rows, width), x.dtype),
+            pltpu.VMEM((n_rows, block // n_rows, width), x.dtype),
+            pltpu.VMEM((block // n_rows, width), x.dtype),
+            pltpu.SemaphoreType.DMA((n_cols,)),
+            pltpu.SemaphoreType.DMA((n_cols,)),
+            pltpu.SemaphoreType.DMA((n_rows,)),
+            pltpu.SemaphoreType.DMA((n_rows,)),
+            pltpu.SemaphoreType.DMA((n_rows,)),
+            pltpu.SemaphoreType.DMA((n_rows,)),
+            pltpu.SemaphoreType.DMA((n_cols,)),
+            pltpu.SemaphoreType.DMA((n_cols,)),
+        ],
+        compiler_params=pltpu.CompilerParams(collective_id=0, has_side_effects=True),
+    )(x.reshape(n_cols, block, width))
+    return out.reshape(rows, width)
 
 
 def body(snapshots, test_matrix):

time: 168 us -> 158 us (0.940)
  blocking collectives: 94.4 us -> 43.9 us
  Pallas kernels: 0 us -> 36.5 us
    pallas_call x0 -> x1, Pallas kernels: none -> 36.5 us  [all_reduce(): pl.pallas_call(functools.partial(all_reduce_kernel, n_rows, n_cols), out_...]
    all_to_all x3 -> x2, blocking collectives: 73.5 us -> 43.9 us  [reduce_scatter(): return lax.all_to_all(chunks, axis, 0, 0, tiled=True).sum(0)]
    all_to_all x1 -> x0, blocking collectives: 20.9 us -> none  [all_reduce(): return lax.all_to_all(spread, axes, 0, 0, tiled=True).reshape(x.shape)]
    unnamed x4 -> x7, local copies, waits for them, and re-layouts: 1.23 us -> 3 us
where the time goes in v4:
time: 158 us; the launch traced here: 155 us
  other arithmetic  48.8 us (31%)
  blocking collectives  43.9 us (28%)
  Pallas kernels  36.5 us (23%)
  matrix products  21.6 us (14%)
  local copies, waits for them, and re-layouts  3.38 us (2%)
    all_to_all x2, blocking collectives, reduce_scatter(): return lax.all_to_all(chunks, axis, 0, 0, tiled=True).sum(0)  43.9 us
    pallas_call x1, Pallas kernels, all_reduce(): pl.pallas_call(functools.partial(all_reduce_kernel, n_rows, n_cols), out_...  36.5 us
    another operation x3, other arithmetic, lower_inverse(): low11 = jnp.linalg.cholesky(gram[:half, :half])  13.2 us
    another operation x3, other arithmetic, lower_inverse(): low22 = jnp.linalg.cholesky(gram[half:, half:] - matmul(low21, low21.T))  12.4 us
    another operation x2, other arithmetic, lower_inverse(): lax.linalg.triangular_solve(low11, identity, left_side=True, lower=True)  11.1 us
    another operation x2, other arithmetic, lower_inverse(): lax.linalg.triangular_solve(low22, identity, left_side=True, lower=True)  10.7 us
    dot_general x1, matrix products, body(): lax.dot_general(snapshots, basis_half, (((0,), (0,)), ((), ())), preferre...  6.55 us
    dot_general x1, matrix products, body(): sketch = jnp.dot(snapshots, test_matrix, preferred_element_type=jnp.float32)  5.73 us

profile of v4, /device:TPU:1, one launch (start us, length us, event | category | flops | bytes accessed | tf_op | source)
XLA Modules:
  0.0 155.1 jit_solution(11432427173458189200)
XLA Ops:
  0.6 0.0 copy-start
  0.6 1.2 copy-done
  1.9 5.7 %fusion.24 = f32[2048,256]{1,0:T(8,128)S(1)} fusion(bf16[2048,2048]{1,0:T(8,128)(2,1)} %param.5, bf16[2048,256]{1,0:T(8,128)(2,1)S(1)} %copy-done), kind=kOutput, calls=%fused_computation.41 | convolution fusion | flops 2147483648 | bytes 11534336 | tf_op jit(solution)/shard_map/dot_general | solution.py:140
  7.6 4.2 %fusion.25 = f32[256,256]{1,0:T(8,128)} fusion(f32[2048,256]{1,0:T(8,128)S(1)} %fusion.24), kind=kOutput, calls=%fused_computation.42 | convolution fusion | flops 1610612736 | bytes 2359296 | tf_op jit(solution)/shard_map/dot_general | solution.py:13
  11.8 36.5 %shard_map.41 = f32[8,32,1,256]{3,2,1,0:T(1,128)} custom-call(f32[8,32,256]{2,1,0:T(8,128)} %bitcast.44), custom_call_target="tpu_custom_call" | custom-call | tf_op jit(solution)/shard_map/pallas_call | solution.py:111
  48.3 1.0 copy.25
  49.3 0.1 copy.26
  49.4 0.6 fusion.23
  50.0 0.7 copy.27
  50.7 12.5 %cholesky.44 = f32[128,128]{1,0:T(8,128)S(1)} custom-call(f32[128,128]{1,0:T(8,128)} %get-tuple-element.5), custom_call_target="Cholesky" | custom-call | tf_op jit(solution)/shard_map/jit(cholesky)/cholesky | solution.py:29
  63.3 0.6 compare_reduce_fusion.1
  64.0 0.7 fusion.12
  64.6 10.4 %custom-call.6 = f32[1,128,128]{1,2,0:T(8,128)} custom-call(f32[1,128,128]{2,1,0:T(8,128)S(1)} %fusion.12), custom_call_target="InvertDiagBlocksLowerTriangular" | custom-call | tf_op jit(solution)/shard_map/triangular_solve/custom-call.0 | solution.py:30
  75.1 1.1 fusion.10
  76.2 0.3 fusion.14
  76.5 0.2 fusion.26
  76.7 1.1 convolution_subtract_fusion
  77.8 0.1 copy.19
  77.9 11.7 %cholesky.55 = f32[128,128]{1,0:T(8,128)S(1)} custom-call(f32[128,128]{1,0:T(8,128)S(1)} %fusion.17), custom_call_target="Cholesky" | custom-call | tf_op jit(solution)/shard_map/jit(cholesky)/cholesky | solution.py:32
  89.7 0.6 compare_reduce_fusion
  90.3 0.7 fusion.13
  91.0 10.0 %custom-call.7 = f32[1,128,128]{1,2,0:T(8,128)S(1)} custom-call(f32[1,128,128]{2,1,0:T(8,128)S(1)} %fusion.13), custom_call_target="InvertDiagBlocksLowerTriangular" | custom-call | tf_op jit(solution)/shard_map/triangular_solve/custom-call.0 | solution.py:33
  101.0 0.3 fusion.8
  101.2 0.1 copy.21
  101.3 0.3 convolution_negate_fusion
  101.6 1.9 %convolution_multiply_fusion = f32[2048,256]{1,0:T(8,128)S(1)} fusion(f32[2048,256]{1,0:T(8,128)S(1)} %fusion.24, f32[128,128]{1,0:T(8,128)S(1)} %fusion.10, f32[128,128]{1,0:T(8,128)S(1)} %copy.21, f32[128,128]{1,0:T(8,128)S(1)} %convolution_negate_fusion), kind=kOutput, calls=%fused_computation | convolution fusion | flops 1611399168 | bytes 4390912 | tf_op jit(solution)/shard_map/dot_general | solution.py:144
  103.6 0.0 copy-start.1
  103.6 6.5 %fusion = f32[256,2048]{1,0:T(8,128)S(1)} fusion(bf16[2048,2048]{1,0:T(8,128)(2,1)} %param.5, f32[2048,256]{1,0:T(8,128)S(1)} %convolution_multiply_fusion), kind=kOutput, calls=%fused_computation.4 | convolution fusion | flops 2148007936 | bytes 12582912 | tf_op jit(solution)/shard_map/dot_general | solution.py:152
  110.1 0.0 copy-done.1
  110.1 0.2 copy.30
  110.3 30.2 %all_to_all.10 = f32[8,256,256]{1,2,0:T(8,128)S(1)} all-to-all(f32[8,256,256]{1,2,0:T(8,128)S(1)} %bitcast.42), channel_id=1, replica_groups=mesh['rows'=32,'cols'=8] {'cols'}, dimensions={0} | all-to-all | bytes 4194304 | tf_op jit(solution)/shard_map/all_to_all | solution.py:41
  140.5 0.1 reduce_sum.18
  140.7 13.8 %all_to_all.11 = f32[32,8,256]{2,1,0:T(8,128)S(1)} all-to-all(f32[32,8,256]{2,1,0:T(8,128)S(1)} %bitcast.43), channel_id=1, replica_groups=mesh['rows'=32,'cols'=8] {'rows'}, dimensions={0} | all-to-all | bytes 524288 | tf_op jit(solution)/shard_map/all_to_all | solution.py:41
  154.5 0.6 broadcast_multiply_fusion
  (5 shorter events, 0.1 us)
Async XLA Ops:
  0.6 1.2 copy-start
  103.6 6.6 %copy-start.1 = (f32[2048,256]{1,0:T(8,128)}, f32[2048,256]{1,0:T(8,128)S(1)}, u32[]{:S(2)}) copy-start(f32[2048,256]{1,0:T(8,128)S(1)} %convolution_multiply_fusion) | copy-start | bytes 6291460

commit v5 on v4

--- a/solution.py
+++ b/solution.py
@@ -130,6 +130,102 @@
         compiler_params=pltpu.CompilerParams(collective_id=0, has_side_effects=True),
     )(x.reshape(n_cols, block, width))
     return out.reshape(rows, width)
+
+
+def projection_kernel(n_rows, n_cols, local_ref, out_ref, from_core, by_chip, from_chip, part, from_row,
+                      send_a, arrive_a, send_b, arrive_b, send_c, arrive_c):
+    me_r = lax.axis_index("rows")
+    me_c = lax.axis_index("cols")
+    core = lax.rem(me_c, 2)
+    chip = me_c // 2
+    partner = me_c + 1 - 2 * core
+    n_chips = n_cols // 2
+    width = local_ref.shape[1] // n_cols
+
+    def columns(c):
+        return pl.ds(pl.multiple_of(c * width, width), width)
+
+    def copy(src, dst, send, arrive, device):
+        return pltpu.make_async_remote_copy(
+            src_ref=src, dst_ref=dst, send_sem=send, recv_sem=arrive,
+            device_id=device, device_id_type=pl.DeviceIdType.MESH,
+        )
+
+    def along(n, mine, step):
+        def visit(i, carry):
+            step(lax.rem(mine + 1 + i, n))
+            return carry
+
+        lax.fori_loop(0, n - 1, visit, 0)
+
+    barrier = pltpu.get_barrier_semaphore()
+    signal = functools.partial(pl.semaphore_signal, barrier, 1, device_id_type=pl.DeviceIdType.MESH)
+    signal(device_id=(me_r, partner))
+    along(n_chips, chip, lambda x: signal(device_id=(me_r, x * 2 + core)))
+    along(n_rows, me_r, lambda r: signal(device_id=(r, me_c)))
+    pl.semaphore_wait(barrier, n_chips + n_rows - 1)
+
+    def swap(x):
+        return copy(local_ref.at[:, columns(x * 2 + 1 - core)], from_core.at[x],
+                    send_a.at[x], arrive_a.at[x], (me_r, partner))
+
+    for x in range(n_chips):
+        swap(x).start()
+    for x in range(n_chips):
+        swap(x).wait_recv()
+    for x in range(n_chips):
+        swap(x).wait_send()
+    for x in range(n_chips):
+        by_chip[x] = local_ref[:, columns(x * 2 + core)] + from_core[x]
+
+    def share(x):
+        return copy(by_chip.at[x], from_chip.at[chip], send_b.at[x], arrive_b.at[chip], (me_r, x * 2 + core))
+
+    along(n_chips, chip, lambda x: share(x).start())
+    from_chip[chip] = by_chip[chip]
+    along(n_chips, chip, lambda x: copy(from_chip.at[x], from_chip.at[x], send_b.at[x], arrive_b.at[x],
+                                        (me_r, x * 2 + core)).wait_recv())
+    along(n_chips, chip, lambda x: share(x).wait_send())
+    part[...] = jnp.sum(from_chip[...], axis=0).reshape(part.shape)
+
+    def scatter(r):
+        return copy(part.at[r], from_row.at[me_r], send_c.at[r], arrive_c.at[me_r], (r, me_c))
+
+    along(n_rows, me_r, lambda r: scatter(r).start())
+    from_row[me_r] = part[me_r]
+    along(n_rows, me_r, lambda r: copy(from_row.at[r], from_row.at[r], send_c.at[r], arrive_c.at[r],
+                                       (r, me_c)).wait_recv())
+    along(n_rows, me_r, lambda r: scatter(r).wait_send())
+    out_ref[...] = jnp.sum(from_row[...], axis=0)
+
+
+def reduce_projection(partial):
+    n_rows = lax.axis_size("rows")
+    n_cols = lax.axis_size("cols")
+    rank, grid = partial.shape
+    width = grid // n_cols
+    share = rank // n_rows
+    n_chips = n_cols // 2
+    return pl.pallas_call(
+        functools.partial(projection_kernel, n_rows, n_cols),
+        out_shape=jax.ShapeDtypeStruct((share, width), partial.dtype),
+        in_specs=[pl.BlockSpec(memory_space=pltpu.VMEM)],
+        out_specs=pl.BlockSpec(memory_space=pltpu.VMEM),
+        scratch_shapes=[
+            pltpu.VMEM((n_chips, rank, width), partial.dtype),
+            pltpu.VMEM((n_chips, rank, width), partial.dtype),
+            pltpu.VMEM((n_chips, rank, width), partial.dtype),
+            pltpu.VMEM((n_rows, share, width), partial.dtype),
+            pltpu.VMEM((n_rows, share, width), partial.dtype),
+            pltpu.SemaphoreType.DMA((n_chips,)),
+            pltpu.SemaphoreType.DMA((n_chips,)),
+            pltpu.SemaphoreType.DMA((n_chips,)),
+            pltpu.SemaphoreType.DMA((n_chips,)),
+            pltpu.SemaphoreType.DMA((n_rows,)),
+            pltpu.SemaphoreType.DMA((n_rows,)),
+        ],
+        compiler_params=pltpu.CompilerParams(collective_id=1, has_side_effects=True),
+    )(partial)
 
 
 def body(snapshots, test_matrix):
@@ -150,10 +246,9 @@
     ) * math.sqrt(total_rows)
     basis_half = basis_full.astype(jnp.bfloat16)
     partial = lax.dot_general(
-        snapshots, basis_half, (((0,), (0,)), ((), ())), preferred_element_type=jnp.float32
+        basis_half, snapshots, (((0,), (0,)), ((), ())), preferred_element_type=jnp.float32
     )
-    grid_part = reduce_scatter(partial, "cols", n_cols)
-    projected = reduce_scatter(grid_part.T, "rows", n_rows)
+    projected = reduce_projection(partial)
     coeffs = projected * (1.0 / math.sqrt(total_rows))
     return (basis_full, coeffs)
 

time: 158 us -> 147 us (0.930); the launches traced: 155 us -> 146 us
  blocking collectives: 43.9 us -> 0 us
  Pallas kernels: 36.5 us -> 69.2 us
  other arithmetic: 48.8 us -> 50.8 us
    all_to_all x2 -> x0, blocking collectives: 43.9 us -> none  [reduce_scatter(): return lax.all_to_all(chunks, axis, 0, 0, tiled=True).sum(0)]
    pallas_call x0 -> x1, Pallas kernels: none -> 32.7 us  [reduce_projection(): pl.pallas_call(functools.partial(projection_kernel, n_rows, n_cols), out_...]
where the time goes in v5:
time: 147 us; the launch traced here: 146 us
  Pallas kernels  69.2 us (47%)
  other arithmetic  50.8 us (35%)
  matrix products  21.4 us (15%)
  local copies, waits for them, and re-layouts  3.86 us (3%)
    pallas_call x1, Pallas kernels, all_reduce(): pl.pallas_call(functools.partial(all_reduce_kernel, n_rows, n_cols), out_...  36.5 us
    pallas_call x1, Pallas kernels, reduce_projection(): pl.pallas_call(functools.partial(projection_kernel, n_rows, n_cols), out_...  32.7 us
    another operation x3, other arithmetic, lower_inverse(): low11 = jnp.linalg.cholesky(gram[:half, :half])  13.2 us
    another operation x2, other arithmetic, lower_inverse(): lax.linalg.triangular_solve(low11, identity, left_side=True, lower=True)  12.6 us
    another operation x3, other arithmetic, lower_inverse(): low22 = jnp.linalg.cholesky(gram[half:, half:] - matmul(low21, low21.T))  12.4 us
    another operation x2, other arithmetic, lower_inverse(): lax.linalg.triangular_solve(low22, identity, left_side=True, lower=True)  10.7 us
    dot_general x1, matrix products, body(): lax.dot_general(basis_half, snapshots, (((0,), (0,)), ((), ())), preferre...  7.14 us
    dot_general x1, matrix products, body(): sketch = jnp.dot(snapshots, test_matrix, preferred_element_type=jnp.float32)  5.73 us

profile of v5, /device:TPU:1, one launch (start us, length us, event | category | flops | bytes accessed | tf_op | source)
XLA Modules:
  0.0 146.0 jit_solution(14413962074809290902)
XLA Ops:
  0.6 0.0 copy-start
  0.6 1.2 copy-done
  1.9 5.7 %fusion.24 = f32[2048,256]{1,0:T(8,128)S(1)} fusion(bf16[2048,2048]{1,0:T(8,128)(2,1)} %param.5, bf16[2048,256]{1,0:T(8,128)(2,1)S(1)} %copy-done), kind=kOutput, calls=%fused_computation.40 | convolution fusion | flops 2147483648 | bytes 11534336 | tf_op jit(solution)/shard_map/dot_general | solution.py:236
  7.6 4.2 %fusion.25 = f32[256,256]{1,0:T(8,128)} fusion(f32[2048,256]{1,0:T(8,128)S(1)} %fusion.24), kind=kOutput, calls=%fused_computation.41 | convolution fusion | flops 1610612736 | bytes 2359296 | tf_op jit(solution)/shard_map/dot_general | solution.py:13
  11.8 36.5 %shard_map.41 = f32[8,32,1,256]{3,2,1,0:T(1,128)} custom-call(f32[8,32,256]{2,1,0:T(8,128)} %bitcast.33), custom_call_target="tpu_custom_call" | custom-call | tf_op jit(solution)/shard_map/pallas_call | solution.py:111
  48.3 1.0 copy.16
  49.3 0.1 copy.17
  49.4 0.6 fusion.23
  50.0 0.1 copy.18
  50.1 12.6 %cholesky.44 = f32[128,128]{1,0:T(8,128)S(1)} custom-call(f32[128,128]{1,0:T(8,128)} %get-tuple-element.5), custom_call_target="Cholesky" | custom-call | tf_op jit(solution)/shard_map/jit(cholesky)/cholesky | solution.py:29
  62.7 0.6 compare_reduce_fusion.1
  63.4 1.3 fusion.12
  64.6 11.3 %custom-call.6 = f32[1,128,128]{1,2,0:T(8,128)} custom-call(f32[1,128,128]{2,1,0:T(8,128)} %fusion.12), custom_call_target="InvertDiagBlocksLowerTriangular" | custom-call | tf_op jit(solution)/shard_map/triangular_solve/custom-call.0 | solution.py:30
  75.9 1.1 fusion.10
  77.0 0.3 fusion.14
  77.3 0.3 convolution_subtract_fusion
  77.6 0.2 fusion.26
  77.8 0.1 copy.13
  77.9 11.7 %cholesky.55 = f32[128,128]{1,0:T(8,128)S(1)} custom-call(f32[128,128]{1,0:T(8,128)S(1)} %fusion.17), custom_call_target="Cholesky" | custom-call | tf_op jit(solution)/shard_map/jit(cholesky)/cholesky | solution.py:32
  89.7 0.6 compare_reduce_fusion
  90.3 0.7 fusion.13
  91.0 10.0 %custom-call.7 = f32[1,128,128]{1,2,0:T(8,128)S(1)} custom-call(f32[1,128,128]{2,1,0:T(8,128)S(1)} %fusion.13), custom_call_target="InvertDiagBlocksLowerTriangular" | custom-call | tf_op jit(solution)/shard_map/triangular_solve/custom-call.0 | solution.py:33
  101.0 0.3 fusion.8
  101.2 0.3 convolution_negate_fusion
  101.5 0.1 copy.14
  101.6 1.9 %convolution_multiply_fusion = f32[2048,256]{1,0:T(8,128)S(1)} fusion(f32[2048,256]{1,0:T(8,128)S(1)} %fusion.24, f32[128,128]{1,0:T(8,128)S(1)} %fusion.10, f32[128,128]{1,0:T(8,128)S(1)} %copy.14, f32[128,128]{1,0:T(8,128)S(1)} %convolution_negate_fusion), kind=kOutput, calls=%fused_computation | convolution fusion | flops 1611399168 | bytes 4390912 | tf_op jit(solution)/shard_map/dot_general | solution.py:240
  103.5 0.0 copy-start.1
  103.6 1.3 copy-done.1
  104.9 7.1 %fusion.local_ref = f32[256,2048]{1,0:T(8,128)} fusion(bf16[2048,2048]{1,0:T(8,128)(2,1)} %param.5, f32[2048,256]{1,0:T(8,128)S(1)} %convolution_multiply_fusion), kind=kOutput, calls=%fused_computation.3 | convolution fusion | flops 2148007936 | bytes 12582912 | tf_op jit(solution)/shard_map/dot_general | solution.py:248
  112.0 32.7 %shard_map.42 = f32[8,256]{1,0:T(8,128)} custom-call(f32[256,2048]{1,0:T(8,128)} %fusion.local_ref), custom_call_target="tpu_custom_call" | custom-call | tf_op jit(solution)/shard_map/pallas_call | solution.py:209
  144.7 1.3 broadcast_multiply_fusion
  (4 shorter events, 0.1 us)
Async XLA Ops:
  0.6 1.2 copy-start
  103.5 1.3 copy-start.1

commit v6 on v5

--- a/solution.py
+++ b/solution.py
@@ -25,12 +25,9 @@
 
 def lower_inverse(gram):
     half = gram.shape[0] // 2
-    identity = jnp.eye(half, dtype=gram.dtype)
-    low11 = jnp.linalg.cholesky(gram[:half, :half])
-    inv11 = lax.linalg.triangular_solve(low11, identity, left_side=True, lower=True)
+    inv11 = factor_inverse(gram[:half, :half])
     low21 = matmul(gram[half:, :half], inv11.T)
-    low22 = jnp.linalg.cholesky(gram[half:, half:] - matmul(low21, low21.T))
-    inv22 = lax.linalg.triangular_solve(low22, identity, left_side=True, lower=True)
+    inv22 = factor_inverse(gram[half:, half:] - matmul(low21, low21.T))
     inv21 = -matmul(inv22, matmul(low21, inv11))
     top = jnp.concatenate([inv11, jnp.zeros_like(inv11)], axis=1)
     return jnp.concatenate([top, jnp.concatenate([inv21, inv22], axis=1)], axis=0)
@@ -226,6 +223,41 @@
         ],
         compiler_params=pltpu.CompilerParams(collective_id=1, has_side_effects=True),
     )(partial)
+
+
+def factor_inverse_kernel(gram_ref, inverse_ref):
+    size = gram_ref.shape[0]
+    sub = lax.broadcasted_iota(jnp.int32, (size, size), 0)
+    lane = lax.broadcasted_iota(jnp.int32, (size, size), 1)
+    lane_row = lax.broadcasted_iota(jnp.int32, (1, size), 1)
+    sub_col = lax.broadcasted_iota(jnp.int32, (size, 1), 0)
+
+    def step(k, carry):
+        work, inverse = carry
+        row = jnp.sum(jnp.where(sub == k, work, 0.0), axis=0, keepdims=True)
+        column = jnp.sum(jnp.where(lane == k, work, 0.0), axis=1, keepdims=True)
+        pivot = jnp.sum(jnp.where(lane_row == k, row, 0.0), axis=1, keepdims=True)
+        scale = lax.rsqrt(pivot)
+        low_row = jnp.where(lane_row >= k, row * scale, 0.0)
+        low_column = jnp.where(sub_col >= k, column * scale, 0.0)
+        work = work - low_column * low_row
+        inverse_row = jnp.sum(jnp.where(sub == k, inverse, 0.0), axis=0, keepdims=True) * scale
+        below = jnp.where(sub_col > k, low_column, 0.0)
+        inverse = jnp.where(sub == k, inverse_row, inverse - below * inverse_row)
+        return work, inverse
+
+    identity = jnp.where(sub == lane, 1.0, 0.0).astype(jnp.float32)
+    _, inverse = lax.fori_loop(0, size, step, (gram_ref[...], identity))
+    inverse_ref[...] = inverse
+
+
+def factor_inverse(gram):
+    return pl.pallas_call(
+        factor_inverse_kernel,
+        out_shape=jax.ShapeDtypeStruct(gram.shape, gram.dtype),
+        in_specs=[pl.BlockSpec(memory_space=pltpu.VMEM)],
+        out_specs=pl.BlockSpec(memory_space=pltpu.VMEM),
+    )(gram)
 
 
 def body(snapshots, test_matrix):

time: 147 us -> 138 us (0.939)
  other arithmetic: 50.8 us -> 1.3 us
  Pallas kernels: 69.2 us -> 107 us
  matrix products: 21.4 us -> 23.9 us
    another operation x10 -> x0, other arithmetic: 48.8 us -> none  [the longest x3 13.2 us: lower_inverse(): low11 = jnp.linalg.cholesky(gram[:half, :half])]
    pallas_call x0 -> x2, Pallas kernels: none -> 37.7 us  [factor_inverse(): pl.pallas_call(factor_inverse_kernel, out_shape=jax.ShapeDtypeStruct(gram...]
    dot_general x4, matrix products: 1.03 us -> 4.09 us  [matmul(): jnp.dot(left, right, precision=lax.Precision.HIGHEST, preferred_element_t...]
    unnamed x7 -> x5, local copies, waits for them, and re-layouts: 3.68 us -> 3.51 us
where the time goes in v6:
time: 138 us; the launch traced here: 137 us
  Pallas kernels  107 us (78%)
  matrix products  23.9 us (17%)
  local copies, waits for them, and re-layouts  4.14 us (3%)
    pallas_call x2, Pallas kernels, factor_inverse(): pl.pallas_call(factor_inverse_kernel, out_shape=jax.ShapeDtypeStruct(gram...  37.7 us
    pallas_call x1, Pallas kernels, all_reduce(): pl.pallas_call(functools.partial(all_reduce_kernel, n_rows, n_cols), out_...  36.5 us
    pallas_call x1, Pallas kernels, reduce_projection(): pl.pallas_call(functools.partial(projection_kernel, n_rows, n_cols), out_...  32.7 us
    dot_general x1, matrix products, body(): lax.dot_general(basis_half, snapshots, (((0,), (0,)), ((), ())), preferre...  7.13 us
    dot_general x1, matrix products, body(): sketch = jnp.dot(snapshots, test_matrix, preferred_element_type=jnp.float32)  5.73 us
    dot_general x1, matrix products, cross_product(): lax.dot_general(left, right, (((0,), (0,)), ((), ())), precision=lax.Prec...  4.19 us
    dot_general x4, matrix products, matmul(): jnp.dot(left, right, precision=lax.Precision.HIGHEST, preferred_element_t...  4.09 us
    unnamed x5, local copies, waits for them, and re-layouts  3.51 us

profile of v6, /device:TPU:1, one launch (start us, length us, event | category | flops | bytes accessed | tf_op | source)
XLA Modules:
  0.0 137.0 jit_solution(16157172329526418094)
XLA Ops:
  0.6 0.0 copy-start
  0.6 1.2 copy-done
  1.9 5.7 %fusion.13 = f32[2048,256]{1,0:T(8,128)S(1)} fusion(bf16[2048,2048]{1,0:T(8,128)(2,1)} %param.2, bf16[2048,256]{1,0:T(8,128)(2,1)S(1)} %copy-done), kind=kOutput, calls=%fused_computation.19 | convolution fusion | flops 2147483648 | bytes 11534336 | tf_op jit(solution)/shard_map/dot_general | solution.py:268
  7.6 4.2 %fusion.14 = f32[256,256]{1,0:T(8,128)} fusion(f32[2048,256]{1,0:T(8,128)S(1)} %fusion.13), kind=kOutput, calls=%fused_computation.20 | convolution fusion | flops 1610612736 | bytes 2359296 | tf_op jit(solution)/shard_map/dot_general | solution.py:13
  11.8 36.5 %shard_map.41 = f32[8,32,1,256]{3,2,1,0:T(1,128)} custom-call(f32[8,32,256]{2,1,0:T(8,128)} %bitcast.15), custom_call_target="tpu_custom_call" | custom-call | tf_op jit(solution)/shard_map/pallas_call | solution.py:108
  48.3 1.0 copy.4
  49.3 0.6 slice.12.gram_ref
  49.9 18.8 %shard_map.42 = f32[128,128]{1,0:T(8,128)} custom-call(f32[128,128]{1,0:T(8,128)} %slice.12.gram_ref), custom_call_target="tpu_custom_call" | custom-call | tf_op jit(solution)/shard_map/pallas_call | solution.py:255
  68.8 1.1 fusion.8
  69.9 0.9 convolution_subtract_fusion.gram_ref
  70.8 18.8 %shard_map.43 = f32[128,128]{1,0:T(8,128)} custom-call(f32[128,128]{1,0:T(8,128)} %convolution_subtract_fusion.gram_ref), custom_call_target="tpu_custom_call" | custom-call | tf_op jit(solution)/shard_map/pallas_call | solution.py:255
  89.6 1.0 fusion.15
  90.6 1.0 convolution_negate_fusion
  91.7 2.8 %convolution_multiply_fusion = f32[2048,256]{1,0:T(8,128)S(1)} fusion(f32[2048,256]{1,0:T(8,128)S(1)} %fusion.13, f32[128,128]{1,0:T(8,128)} %shard_map.42, f32[128,128]{1,0:T(8,128)} %shard_map.43, f32[128,128]{1,0:T(8,128)S(1)} %convolution_negate_fusion), kind=kOutput, calls=%fused_computation | convolution fusion | flops 1611399168 | bytes 4390912 | tf_op jit(solution)/shard_map/dot_general | solution.py:272
  94.5 0.0 copy-start.1
  94.5 1.3 copy-done.1
  95.8 7.1 %fusion.local_ref = f32[256,2048]{1,0:T(8,128)} fusion(bf16[2048,2048]{1,0:T(8,128)(2,1)} %param.2, f32[2048,256]{1,0:T(8,128)S(1)} %convolution_multiply_fusion), kind=kOutput, calls=%fused_computation.3 | convolution fusion | flops 2148007936 | bytes 12582912 | tf_op jit(solution)/shard_map/dot_general | solution.py:280
  102.9 32.7 %shard_map.44 = f32[8,256]{1,0:T(8,128)} custom-call(f32[256,2048]{1,0:T(8,128)} %fusion.local_ref), custom_call_target="tpu_custom_call" | custom-call | tf_op jit(solution)/shard_map/pallas_call | solution.py:206
  135.7 1.3 broadcast_multiply_fusion
Async XLA Ops:
  0.6 1.2 copy-start
  94.5 1.3 copy-start.1

commit v7 on v6

--- a/solution.py
+++ b/solution.py
@@ -225,7 +225,7 @@
     )(partial)
 
 
-def factor_inverse_kernel(gram_ref, inverse_ref):
+def factor_inverse_kernel(gram_ref, inverse_ref, work_ref):
     size = gram_ref.shape[0]
     sub = lax.broadcasted_iota(jnp.int32, (size, size), 0)
     lane = lax.broadcasted_iota(jnp.int32, (size, size), 1)
@@ -233,22 +233,23 @@
     sub_col = lax.broadcasted_iota(jnp.int32, (size, 1), 0)
 
     def step(k, carry):
-        work, inverse = carry
-        row = jnp.sum(jnp.where(sub == k, work, 0.0), axis=0, keepdims=True)
+        row = work_ref[pl.ds(k, 1), :]
+        work = work_ref[...]
         column = jnp.sum(jnp.where(lane == k, work, 0.0), axis=1, keepdims=True)
         pivot = jnp.sum(jnp.where(lane_row == k, row, 0.0), axis=1, keepdims=True)
         scale = lax.rsqrt(pivot)
         low_row = jnp.where(lane_row >= k, row * scale, 0.0)
         low_column = jnp.where(sub_col >= k, column * scale, 0.0)
-        work = work - low_column * low_row
-        inverse_row = jnp.sum(jnp.where(sub == k, inverse, 0.0), axis=0, keepdims=True) * scale
+        work_ref[...] = work - low_column * low_row
+        inverse_row = inverse_ref[pl.ds(k, 1), :] * scale
         below = jnp.where(sub_col > k, low_column, 0.0)
-        inverse = jnp.where(sub == k, inverse_row, inverse - below * inverse_row)
-        return work, inverse
-
-    identity = jnp.where(sub == lane, 1.0, 0.0).astype(jnp.float32)
-    _, inverse = lax.fori_loop(0, size, step, (gram_ref[...], identity))
-    inverse_ref[...] = inverse
+        inverse = inverse_ref[...]
+        inverse_ref[...] = jnp.where(sub == k, inverse_row, inverse - below * inverse_row)
+        return carry
+
+    work_ref[...] = gram_ref[...]
+    inverse_ref[...] = jnp.where(sub == lane, 1.0, 0.0).astype(jnp.float32)
+    lax.fori_loop(0, size, step, 0)
 
 
 def factor_inverse(gram):
@@ -257,6 +258,7 @@
         out_shape=jax.ShapeDtypeStruct(gram.shape, gram.dtype),
         in_specs=[pl.BlockSpec(memory_space=pltpu.VMEM)],
         out_specs=pl.BlockSpec(memory_space=pltpu.VMEM),
+        scratch_shapes=[pltpu.VMEM(gram.shape, gram.dtype)],
     )(gram)
 
 

time: 138 us -> 132 us (0.957)
  Pallas kernels: 107 us -> 101 us
    pallas_call x2, Pallas kernels: 37.7 us -> 31.8 us  [factor_inverse(): pl.pallas_call(factor_inverse_kernel, out_shape=jax.ShapeDtypeStruct(gram...]
where the time goes in v7:
time: 132 us; the launch traced here: 131 us
  Pallas kernels  101 us (77%)
  matrix products  23.9 us (18%)
  local copies, waits for them, and re-layouts  4.14 us (3%)
    pallas_call x1, Pallas kernels, all_reduce(): pl.pallas_call(functools.partial(all_reduce_kernel, n_rows, n_cols), out_...  36.5 us
    pallas_call x1, Pallas kernels, reduce_projection(): pl.pallas_call(functools.partial(projection_kernel, n_rows, n_cols), out_...  32.7 us
    pallas_call x2, Pallas kernels, factor_inverse(): pl.pallas_call(factor_inverse_kernel, out_shape=jax.ShapeDtypeStruct(gram...  31.8 us
    dot_general x1, matrix products, body(): lax.dot_general(basis_half, snapshots, (((0,), (0,)), ((), ())), preferre...  7.13 us
    dot_general x1, matrix products, body(): sketch = jnp.dot(snapshots, test_matrix, preferred_element_type=jnp.float32)  5.73 us
    dot_general x1, matrix products, cross_product(): lax.dot_general(left, right, (((0,), (0,)), ((), ())), precision=lax.Prec...  4.19 us
    dot_general x4, matrix products, matmul(): jnp.dot(left, right, precision=lax.Precision.HIGHEST, preferred_element_t...  4.09 us
    unnamed x5, local copies, waits for them, and re-layouts  3.51 us

profile of v7, /device:TPU:1, one launch (start us, length us, event | category | flops | bytes accessed | tf_op | source)
XLA Modules:
  0.0 131.1 jit_solution(7369502695621489915)
XLA Ops:
  0.6 0.0 copy-start
  0.6 1.2 copy-done
  1.9 5.7 %fusion.13 = f32[2048,256]{1,0:T(8,128)S(1)} fusion(bf16[2048,2048]{1,0:T(8,128)(2,1)} %param.2, bf16[2048,256]{1,0:T(8,128)(2,1)S(1)} %copy-done), kind=kOutput, calls=%fused_computation.19 | convolution fusion | flops 2147483648 | bytes 11534336 | tf_op jit(solution)/shard_map/dot_general | solution.py:270
  7.6 4.2 %fusion.14 = f32[256,256]{1,0:T(8,128)} fusion(f32[2048,256]{1,0:T(8,128)S(1)} %fusion.13), kind=kOutput, calls=%fused_computation.20 | convolution fusion | flops 1610612736 | bytes 2359296 | tf_op jit(solution)/shard_map/dot_general | solution.py:13
  11.8 36.5 %shard_map.41 = f32[8,32,1,256]{3,2,1,0:T(1,128)} custom-call(f32[8,32,256]{2,1,0:T(8,128)} %bitcast.15), custom_call_target="tpu_custom_call" | custom-call | tf_op jit(solution)/shard_map/pallas_call | solution.py:108
  48.3 1.0 copy.4
  49.3 0.6 slice.12.gram_ref
  49.9 15.9 %shard_map.42 = f32[128,128]{1,0:T(8,128)} custom-call(f32[128,128]{1,0:T(8,128)} %slice.12.gram_ref), custom_call_target="tpu_custom_call" | custom-call | tf_op jit(solution)/shard_map/pallas_call | solution.py:256
  65.8 1.1 fusion.8
  66.9 0.9 convolution_subtract_fusion.gram_ref
  67.8 15.9 %shard_map.43 = f32[128,128]{1,0:T(8,128)} custom-call(f32[128,128]{1,0:T(8,128)} %convolution_subtract_fusion.gram_ref), custom_call_target="tpu_custom_call" | custom-call | tf_op jit(solution)/shard_map/pallas_call | solution.py:256
  83.7 1.0 fusion.15
  84.8 1.0 convolution_negate_fusion
  85.8 2.8 %convolution_multiply_fusion = f32[2048,256]{1,0:T(8,128)S(1)} fusion(f32[2048,256]{1,0:T(8,128)S(1)} %fusion.13, f32[128,128]{1,0:T(8,128)} %shard_map.42, f32[128,128]{1,0:T(8,128)} %shard_map.43, f32[128,128]{1,0:T(8,128)S(1)} %convolution_negate_fusion), kind=kOutput, calls=%fused_computation | convolution fusion | flops 1611399168 | bytes 4390912 | tf_op jit(solution)/shard_map/dot_general | solution.py:274
  88.6 0.0 copy-start.1
  88.6 1.3 copy-done.1
  89.9 7.1 %fusion.local_ref = f32[256,2048]{1,0:T(8,128)} fusion(bf16[2048,2048]{1,0:T(8,128)(2,1)} %param.2, f32[2048,256]{1,0:T(8,128)S(1)} %convolution_multiply_fusion), kind=kOutput, calls=%fused_computation.3 | convolution fusion | flops 2148007936 | bytes 12582912 | tf_op jit(solution)/shard_map/dot_general | solution.py:282
  97.1 32.7 %shard_map.44 = f32[8,256]{1,0:T(8,128)} custom-call(f32[256,2048]{1,0:T(8,128)} %fusion.local_ref), custom_call_target="tpu_custom_call" | custom-call | tf_op jit(solution)/shard_map/pallas_call | solution.py:206
  129.8 1.3 broadcast_multiply_fusion
Async XLA Ops:
  0.6 1.2 copy-start
  88.6 1.3 %copy-start.1 = (f32[2048,256]{1,0:T(8,128)}, f32[2048,256]{1,0:T(8,128)S(1)}, u32[]{:S(2)}) copy-start(f32[2048,256]{1,0:T(8,128)S(1)} %convolution_multiply_fusion) | copy-start | bytes 6291460

commit v8 on v7

--- a/solution.py
+++ b/solution.py
@@ -21,16 +21,6 @@
 
 def matmul(left, right):
     return jnp.dot(left, right, precision=lax.Precision.HIGHEST, preferred_element_type=jnp.float32)
-
-
-def lower_inverse(gram):
-    half = gram.shape[0] // 2
-    inv11 = factor_inverse(gram[:half, :half])
-    low21 = matmul(gram[half:, :half], inv11.T)
-    inv22 = factor_inverse(gram[half:, half:] - matmul(low21, low21.T))
-    inv21 = -matmul(inv22, matmul(low21, inv11))
-    top = jnp.concatenate([inv11, jnp.zeros_like(inv11)], axis=1)
-    return jnp.concatenate([top, jnp.concatenate([inv21, inv22], axis=1)], axis=0)
 
 
 def reduce_scatter(x, axis, n):
@@ -225,8 +215,8 @@
     )(partial)
 
 
-def factor_inverse_kernel(gram_ref, inverse_ref, work_ref):
-    size = gram_ref.shape[0]
+def factor_inverse_block(gram, inverse_ref, work_ref):
+    size = gram.shape[0]
     sub = lax.broadcasted_iota(jnp.int32, (size, size), 0)
     lane = lax.broadcasted_iota(jnp.int32, (size, size), 1)
     lane_row = lax.broadcasted_iota(jnp.int32, (1, size), 1)
@@ -247,18 +237,40 @@
         inverse_ref[...] = jnp.where(sub == k, inverse_row, inverse - below * inverse_row)
         return carry
 
-    work_ref[...] = gram_ref[...]
+    work_ref[...] = gram
     inverse_ref[...] = jnp.where(sub == lane, 1.0, 0.0).astype(jnp.float32)
     lax.fori_loop(0, size, step, 0)
 
 
-def factor_inverse(gram):
+def nt(left, right):
+    return lax.dot_general(
+        left, right, (((1,), (1,)), ((), ())),
+        precision=lax.Precision.HIGHEST, preferred_element_type=jnp.float32,
+    )
+
+
+def lower_inverse_kernel(gram_ref, out_ref, first, second, work_ref):
+    half = gram_ref.shape[0] // 2
+    factor_inverse_block(gram_ref[:half, :half], first, work_ref)
+    inv11 = first[...]
+    low21 = nt(gram_ref[half:, :half], inv11)
+    factor_inverse_block(gram_ref[half:, half:] - nt(low21, low21), second, work_ref)
+    inv22 = second[...]
+    out_ref[:half, :half] = inv11
+    out_ref[:half, half:] = jnp.zeros_like(inv11)
+    out_ref[half:, :half] = -matmul(inv22, matmul(low21, inv11))
+    out_ref[half:, half:] = inv22
+
+
+def lower_inverse(gram):
+    half = gram.shape[0] // 2
+    block = pltpu.VMEM((half, half), gram.dtype)
     return pl.pallas_call(
-        factor_inverse_kernel,
+        lower_inverse_kernel,
         out_shape=jax.ShapeDtypeStruct(gram.shape, gram.dtype),
         in_specs=[pl.BlockSpec(memory_space=pltpu.VMEM)],
         out_specs=pl.BlockSpec(memory_space=pltpu.VMEM),
-        scratch_shapes=[pltpu.VMEM(gram.shape, gram.dtype)],
+        scratch_shapes=[block, block, block],
     )(gram)
 
 

time: 132 us -> 128 us (0.970)
  matrix products: 23.9 us -> 19.9 us
    dot_general x4 -> x0, matrix products: 4.09 us -> none  [matmul(): jnp.dot(left, right, precision=lax.Precision.HIGHEST, preferred_element_t...]
    pallas_call x2 -> x1, Pallas kernels: 31.8 us -> 32.3 us  [lower_inverse(): pl.pallas_call(lower_inverse_kernel, out_shape=jax.ShapeDtypeStruct(gram....]
where the time goes in v8:
time: 128 us
  Pallas kernels  102 us (80%)
  matrix products  19.9 us (16%)
  local copies, waits for them, and re-layouts  4.21 us (3%)
  other arithmetic  1.3 us (1%)
    pallas_call x1, Pallas kernels, all_reduce(): pl.pallas_call(functools.partial(all_reduce_kernel, n_rows, n_cols), out_...  36.5 us
    pallas_call x1, Pallas kernels, reduce_projection(): pl.pallas_call(functools.partial(projection_kernel, n_rows, n_cols), out_...  32.7 us
    pallas_call x1, Pallas kernels, lower_inverse(): pl.pallas_call(lower_inverse_kernel, out_shape=jax.ShapeDtypeStruct(gram....  32.3 us
    dot_general x1, matrix products, body(): lax.dot_general(basis_half, snapshots, (((0,), (0,)), ((), ())), preferre...  7.13 us
    dot_general x1, matrix products, body(): sketch = jnp.dot(snapshots, test_matrix, preferred_element_type=jnp.float32)  5.73 us
    unnamed x5, local copies, waits for them, and re-layouts  4.21 us
    dot_general x1, matrix products, cross_product(): lax.dot_general(left, right, (((0,), (0,)), ((), ())), precision=lax.Prec...  4.19 us
    dot_general x1, matrix products, body(): lax.dot_general(sketch, inverse_low, (((1,), (1,)), ((), ())), precision=...  2.87 us

profile of v8, /device:TPU:1, one launch (start us, length us, event | category | flops | bytes accessed | tf_op | source)
XLA Modules:
  0.0 127.7 jit_solution(2068820177644705949)
XLA Ops:
  0.6 0.0 copy-start
  0.6 1.2 copy-done
  1.9 5.7 %fusion.2 = f32[2048,256]{1,0:T(8,128)S(1)} fusion(bf16[2048,2048]{1,0:T(8,128)(2,1)} %param.2, bf16[2048,256]{1,0:T(8,128)(2,1)S(1)} %copy-done), kind=kOutput, calls=%fused_computation.4 | convolution fusion | flops 2147483648 | bytes 11534336 | tf_op jit(solution)/shard_map/dot_general | solution.py:282
  7.6 4.2 %fusion.3 = f32[256,256]{1,0:T(8,128)} fusion(f32[2048,256]{1,0:T(8,128)S(1)} %fusion.2), kind=kOutput, calls=%fused_computation.5 | convolution fusion | flops 1610612736 | bytes 2359296 | tf_op jit(solution)/shard_map/dot_general | solution.py:13
  11.8 36.5 %shard_map.41 = f32[8,32,1,256]{3,2,1,0:T(1,128)} custom-call(f32[8,32,256]{2,1,0:T(8,128)} %bitcast.9), custom_call_target="tpu_custom_call" | custom-call | tf_op jit(solution)/shard_map/pallas_call | solution.py:98
  48.3 1.7 %copy.4 = f32[8,32,1,256]{3,1,2,0:T(8,128)} copy(f32[8,32,1,256]{3,2,1,0:T(1,128)} %shard_map.41) | data formatting | bytes 524288
  50.0 32.3 %shard_map.42 = f32[256,256]{1,0:T(8,128)} custom-call(f32[256,256]{1,0:T(8,128)} %bitcast.10), custom_call_target="tpu_custom_call" | custom-call | tf_op jit(solution)/shard_map/pallas_call | solution.py:268
  82.3 2.9 %convolution_multiply_fusion = f32[2048,256]{1,0:T(8,128)S(1)} fusion(f32[2048,256]{1,0:T(8,128)S(1)} %fusion.2, f32[256,256]{1,0:T(8,128)} %shard_map.42), kind=kOutput, calls=%fused_computation | convolution fusion | flops 1611137024 | bytes 4456448 | tf_op jit(solution)/shard_map/dot_general | solution.py:286
  85.2 0.0 copy-start.1
  85.2 1.3 %copy-done.1 = f32[2048,256]{1,0:T(8,128)} copy-done((f32[2048,256]{1,0:T(8,128)}, f32[2048,256]{1,0:T(8,128)S(1)}, u32[]{:S(2)}) %copy-start.1) | copy-done | bytes 2097176
  86.5 7.1 %fusion.local_ref = f32[256,2048]{1,0:T(8,128)} fusion(bf16[2048,2048]{1,0:T(8,128)(2,1)} %param.2, f32[2048,256]{1,0:T(8,128)S(1)} %convolution_multiply_fusion), kind=kOutput, calls=%fused_computation.1 | convolution fusion | flops 2148007936 | bytes 12582912 | tf_op jit(solution)/shard_map/dot_general | solution.py:294
  93.7 32.7 %shard_map.43 = f32[8,256]{1,0:T(8,128)} custom-call(f32[256,2048]{1,0:T(8,128)} %fusion.local_ref), custom_call_target="tpu_custom_call" | custom-call | tf_op jit(solution)/shard_map/pallas_call | solution.py:196
  126.4 1.3 %broadcast_multiply_fusion = f32[8,256]{1,0:T(8,128)} fusion(f32[8,256]{1,0:T(8,128)} %shard_map.43), kind=kLoop, calls=%fused_computation.3 | loop fusion | flops 2048 | bytes 16384 | tf_op jit(solution)/shard_map/mul | solution.py:298
Async XLA Ops:
  0.6 1.2 copy-start
  85.2 1.3 %copy-start.1 = (f32[2048,256]{1,0:T(8,128)}, f32[2048,256]{1,0:T(8,128)S(1)}, u32[]{:S(2)}) copy-start(f32[2048,256]{1,0:T(8,128)S(1)} %convolution_multiply_fusion) | copy-start | bytes 6291460

commit v9 on v8

--- a/solution.py
+++ b/solution.py
@@ -28,7 +28,7 @@
     return lax.all_to_all(chunks, axis, 0, 0, tiled=True).sum(0)
 
 
-def all_reduce_kernel(n_rows, n_cols, local_ref, out_ref, recv1, part, recv2, total,
+def all_reduce_kernel(n_rows, n_cols, local_ref, out_ref, recv1, part, recv2, total, rows_in,
                       send1, arrive1, send2, arrive2, send3, arrive3, send4, arrive4):
     me_r = lax.axis_index("rows")
     me_c = lax.axis_index("cols")
@@ -75,18 +75,24 @@
     total[...] = jnp.sum(recv2[...], axis=0)
 
     def gather3(r):
-        return copy(total, out_ref.at[me_c, me_r], send3.at[r], arrive3.at[me_r], (r, me_c))
+        return copy(total, rows_in.at[me_r], send3.at[r], arrive3.at[me_r], (r, me_c))
 
     along(n_rows, me_r, lambda r: gather3(r).start())
-    out_ref[me_c, me_r] = total[...]
-    along(n_rows, me_r, lambda r: copy(out_ref.at[me_c, r], out_ref.at[me_c, r], send3.at[r], arrive3.at[r], (r, me_c)).wait_recv())
+    rows_in[me_r] = total[...]
+    along(n_rows, me_r, lambda r: copy(rows_in.at[r], rows_in.at[r], send3.at[r], arrive3.at[r], (r, me_c)).wait_recv())
     along(n_rows, me_r, lambda r: gather3(r).wait_send())
+    block = n_rows * share
+
+    def rows_of(c):
+        return pl.ds(pl.multiple_of(c * block, block), block)
+
+    out_ref[rows_of(me_c), :] = jnp.concatenate([rows_in[r] for r in range(n_rows)], axis=0)
 
     def gather4(c):
-        return copy(out_ref.at[me_c], out_ref.at[me_c], send4.at[c], arrive4.at[me_c], (me_r, c))
+        return copy(out_ref.at[rows_of(me_c)], out_ref.at[rows_of(me_c)], send4.at[c], arrive4.at[me_c], (me_r, c))
 
     along(n_cols, me_c, lambda c: gather4(c).start())
-    along(n_cols, me_c, lambda c: copy(out_ref.at[c], out_ref.at[c], send4.at[c], arrive4.at[c], (me_r, c)).wait_recv())
+    along(n_cols, me_c, lambda c: copy(out_ref.at[rows_of(c)], out_ref.at[rows_of(c)], send4.at[c], arrive4.at[c], (me_r, c)).wait_recv())
     along(n_cols, me_c, lambda c: gather4(c).wait_send())
 
 
@@ -97,7 +103,7 @@
     block = rows // n_cols
     out = pl.pallas_call(
         functools.partial(all_reduce_kernel, n_rows, n_cols),
-        out_shape=jax.ShapeDtypeStruct((n_cols, n_rows, block // n_rows, width), x.dtype),
+        out_shape=jax.ShapeDtypeStruct((rows, width), x.dtype),
         in_specs=[pl.BlockSpec(memory_space=pltpu.VMEM)],
         out_specs=pl.BlockSpec(memory_space=pltpu.VMEM),
         scratch_shapes=[
@@ -105,6 +111,7 @@
             pltpu.VMEM((n_rows, block // n_rows, width), x.dtype),
             pltpu.VMEM((n_rows, block // n_rows, width), x.dtype),
             pltpu.VMEM((block // n_rows, width), x.dtype),
+            pltpu.VMEM((n_rows, block // n_rows, width), x.dtype),
             pltpu.SemaphoreType.DMA((n_cols,)),
             pltpu.SemaphoreType.DMA((n_cols,)),
             pltpu.SemaphoreType.DMA((n_rows,)),
@@ -116,7 +123,7 @@
         ],
         compiler_params=pltpu.CompilerParams(collective_id=0, has_side_effects=True),
     )(x.reshape(n_cols, block, width))
-    return out.reshape(rows, width)
+    return out
 
 
 def projection_kernel(n_rows, n_cols, local_ref, out_ref, from_core, by_chip, from_chip, part, from_row,

time: 128 us -> 126 us (0.984)
  local copies, waits for them, and re-layouts: 4.21 us -> 2.54 us
    unnamed x5 -> x4, local copies, waits for them, and re-layouts: 4.21 us -> 2.54 us
where the time goes in v9:
time: 126 us
  Pallas kernels  102 us (81%)
  matrix products  19.9 us (16%)
  local copies, waits for them, and re-layouts  2.54 us (2%)
  other arithmetic  1.3 us (1%)
    pallas_call x1, Pallas kernels, all_reduce(): pl.pallas_call(functools.partial(all_reduce_kernel, n_rows, n_cols), out_...  36.5 us
    pallas_call x1, Pallas kernels, reduce_projection(): pl.pallas_call(functools.partial(projection_kernel, n_rows, n_cols), out_...  32.7 us
    pallas_call x1, Pallas kernels, lower_inverse(): pl.pallas_call(lower_inverse_kernel, out_shape=jax.ShapeDtypeStruct(gram....  32.4 us
    dot_general x1, matrix products, body(): lax.dot_general(basis_half, snapshots, (((0,), (0,)), ((), ())), preferre...  7.13 us
    dot_general x1, matrix products, body(): sketch = jnp.dot(snapshots, test_matrix, preferred_element_type=jnp.float32)  5.73 us
    dot_general x1, matrix products, cross_product(): lax.dot_general(left, right, (((0,), (0,)), ((), ())), precision=lax.Prec...  4.19 us
    dot_general x1, matrix products, body(): lax.dot_general(sketch, inverse_low, (((1,), (1,)), ((), ())), precision=...  2.88 us
    unnamed x4, local copies, waits for them, and re-layouts  2.54 us

profile of v9, /device:TPU:1, one launch (start us, length us, event | category | flops | bytes accessed | tf_op | source)
XLA Modules:
  0.0 126.0 jit_solution(10852774219429885251)
XLA Ops:
  0.6 0.0 copy-start
  0.6 1.2 copy-done
  1.9 5.7 %fusion.2 = f32[2048,256]{1,0:T(8,128)S(1)} fusion(bf16[2048,2048]{1,0:T(8,128)(2,1)} %param.2, bf16[2048,256]{1,0:T(8,128)(2,1)S(1)} %copy-done), kind=kOutput, calls=%fused_computation.4 | convolution fusion | flops 2147483648 | bytes 11534336 | tf_op jit(solution)/shard_map/dot_general | solution.py:289
  7.6 4.2 %fusion.3 = f32[256,256]{1,0:T(8,128)} fusion(f32[2048,256]{1,0:T(8,128)S(1)} %fusion.2), kind=kOutput, calls=%fused_computation.5 | convolution fusion | flops 1610612736 | bytes 2359296 | tf_op jit(solution)/shard_map/dot_general | solution.py:13
  11.8 36.5 %shard_map.41.gram_ref = f32[256,256]{1,0:T(8,128)} custom-call(f32[8,32,256]{2,1,0:T(8,128)} %bitcast.8), custom_call_target="tpu_custom_call" | custom-call | tf_op jit(solution)/shard_map/pallas_call | solution.py:104
  48.3 32.4 %shard_map.42 = f32[256,256]{1,0:T(8,128)} custom-call(f32[256,256]{1,0:T(8,128)} %shard_map.41.gram_ref), custom_call_target="tpu_custom_call" | custom-call | tf_op jit(solution)/shard_map/pallas_call | solution.py:275
  80.7 2.9 %convolution_multiply_fusion = f32[2048,256]{1,0:T(8,128)S(1)} fusion(f32[2048,256]{1,0:T(8,128)S(1)} %fusion.2, f32[256,256]{1,0:T(8,128)} %shard_map.42), kind=kOutput, calls=%fused_computation | convolution fusion | flops 1611137024 | bytes 4456448 | tf_op jit(solution)/shard_map/dot_general | solution.py:293
  83.6 0.0 copy-start.1
  83.6 1.3 %copy-done.1 = f32[2048,256]{1,0:T(8,128)} copy-done((f32[2048,256]{1,0:T(8,128)}, f32[2048,256]{1,0:T(8,128)S(1)}, u32[]{:S(2)}) %copy-start.1) | copy-done | bytes 2097176
  84.9 7.1 %fusion.local_ref = f32[256,2048]{1,0:T(8,128)} fusion(bf16[2048,2048]{1,0:T(8,128)(2,1)} %param.2, f32[2048,256]{1,0:T(8,128)S(1)} %convolution_multiply_fusion), kind=kOutput, calls=%fused_computation.1 | convolution fusion | flops 2148007936 | bytes 12582912 | tf_op jit(solution)/shard_map/dot_general | solution.py:301
  92.0 32.7 %shard_map.43 = f32[8,256]{1,0:T(8,128)} custom-call(f32[256,2048]{1,0:T(8,128)} %fusion.local_ref), custom_call_target="tpu_custom_call" | custom-call | tf_op jit(solution)/shard_map/pallas_call | solution.py:203
  124.7 1.3 %broadcast_multiply_fusion = f32[8,256]{1,0:T(8,128)} fusion(f32[8,256]{1,0:T(8,128)} %shard_map.43), kind=kLoop, calls=%fused_computation.3 | loop fusion | flops 2048 | bytes 16384 | tf_op jit(solution)/shard_map/mul | solution.py:305
Async XLA Ops:
  0.6 1.2 copy-start
  83.6 1.3 %copy-start.1 = (f32[2048,256]{1,0:T(8,128)}, f32[2048,256]{1,0:T(8,128)S(1)}, u32[]{:S(2)}) copy-start(f32[2048,256]{1,0:T(8,128)S(1)} %convolution_multiply_fusion) | copy-start | bytes 6291460

commit v10 on v9

--- a/solution.py
+++ b/solution.py
@@ -163,19 +163,19 @@
         return copy(local_ref.at[:, columns(x * 2 + 1 - core)], from_core.at[x],
                     send_a.at[x], arrive_a.at[x], (me_r, partner))
 
-    for x in range(n_chips):
-        swap(x).start()
-    for x in range(n_chips):
-        swap(x).wait_recv()
-    for x in range(n_chips):
-        swap(x).wait_send()
-    for x in range(n_chips):
-        by_chip[x] = local_ref[:, columns(x * 2 + core)] + from_core[x]
-
     def share(x):
         return copy(by_chip.at[x], from_chip.at[chip], send_b.at[x], arrive_b.at[chip], (me_r, x * 2 + core))
 
-    along(n_chips, chip, lambda x: share(x).start())
+    order = [lax.rem(chip + 1 + i, n_chips) for i in range(n_chips)]
+    for x in order:
+        swap(x).start()
+    for i, x in enumerate(order):
+        swap(x).wait_recv()
+        by_chip[x] = local_ref[:, columns(x * 2 + core)] + from_core[x]
+        if i < n_chips - 1:
+            share(x).start()
+    for x in order:
+        swap(x).wait_send()
     from_chip[chip] = by_chip[chip]
     along(n_chips, chip, lambda x: copy(from_chip.at[x], from_chip.at[x], send_b.at[x], arrive_b.at[x],
                                         (me_r, x * 2 + core)).wait_recv())

time: 126 us -> 126 us (level)
  no operation moved by 1% of the time
where the time goes in v10:
time: 126 us; the launch traced here: 125 us
  Pallas kernels  101 us (80%)
  matrix products  19.9 us (16%)
  local copies, waits for them, and re-layouts  2.54 us (2%)
  other arithmetic  1.3 us (1%)
    pallas_call x1, Pallas kernels, all_reduce(): pl.pallas_call(functools.partial(all_reduce_kernel, n_rows, n_cols), out_...  36.5 us
    pallas_call x1, Pallas kernels, lower_inverse(): pl.pallas_call(lower_inverse_kernel, out_shape=jax.ShapeDtypeStruct(gram....  32.4 us
    pallas_call x1, Pallas kernels, reduce_projection(): pl.pallas_call(functools.partial(projection_kernel, n_rows, n_cols), out_...  32 us
    dot_general x1, matrix products, body(): lax.dot_general(basis_half, snapshots, (((0,), (0,)), ((), ())), preferre...  7.13 us
    dot_general x1, matrix products, body(): sketch = jnp.dot(snapshots, test_matrix, preferred_element_type=jnp.float32)  5.73 us
    dot_general x1, matrix products, cross_product(): lax.dot_general(left, right, (((0,), (0,)), ((), ())), precision=lax.Prec...  4.19 us
    dot_general x1, matrix products, body(): lax.dot_general(sketch, inverse_low, (((1,), (1,)), ((), ())), precision=...  2.88 us
    unnamed x4, local copies, waits for them, and re-layouts  2.54 us

profile of v10, /device:TPU:1, one launch (start us, length us, event | category | flops | bytes accessed | tf_op | source)
XLA Modules:
  0.0 125.4 jit_solution(18330372337639160362)
XLA Ops:
  0.6 0.0 copy-start
  0.6 1.2 copy-done
  1.9 5.7 %fusion.2 = f32[2048,256]{1,0:T(8,128)S(1)} fusion(bf16[2048,2048]{1,0:T(8,128)(2,1)} %param.2, bf16[2048,256]{1,0:T(8,128)(2,1)S(1)} %copy-done), kind=kOutput, calls=%fused_computation.4 | convolution fusion | flops 2147483648 | bytes 11534336 | tf_op jit(solution)/shard_map/dot_general | solution.py:289
  7.6 4.2 %fusion.3 = f32[256,256]{1,0:T(8,128)} fusion(f32[2048,256]{1,0:T(8,128)S(1)} %fusion.2), kind=kOutput, calls=%fused_computation.5 | convolution fusion | flops 1610612736 | bytes 2359296 | tf_op jit(solution)/shard_map/dot_general | solution.py:13
  11.8 36.5 %shard_map.41.gram_ref = f32[256,256]{1,0:T(8,128)} custom-call(f32[8,32,256]{2,1,0:T(8,128)} %bitcast.8), custom_call_target="tpu_custom_call" | custom-call | tf_op jit(solution)/shard_map/pallas_call | solution.py:104
  48.3 32.4 %shard_map.42 = f32[256,256]{1,0:T(8,128)} custom-call(f32[256,256]{1,0:T(8,128)} %shard_map.41.gram_ref), custom_call_target="tpu_custom_call" | custom-call | tf_op jit(solution)/shard_map/pallas_call | solution.py:275
  80.7 2.9 %convolution_multiply_fusion = f32[2048,256]{1,0:T(8,128)S(1)} fusion(f32[2048,256]{1,0:T(8,128)S(1)} %fusion.2, f32[256,256]{1,0:T(8,128)} %shard_map.42), kind=kOutput, calls=%fused_computation | convolution fusion | flops 1611137024 | bytes 4456448 | tf_op jit(solution)/shard_map/dot_general | solution.py:293
  83.6 0.0 copy-start.1
  83.6 1.3 %copy-done.1 = f32[2048,256]{1,0:T(8,128)} copy-done((f32[2048,256]{1,0:T(8,128)}, f32[2048,256]{1,0:T(8,128)S(1)}, u32[]{:S(2)}) %copy-start.1) | copy-done | bytes 2097176
  84.9 7.1 %fusion.local_ref = f32[256,2048]{1,0:T(8,128)} fusion(bf16[2048,2048]{1,0:T(8,128)(2,1)} %param.2, f32[2048,256]{1,0:T(8,128)S(1)} %convolution_multiply_fusion), kind=kOutput, calls=%fused_computation.1 | convolution fusion | flops 2148007936 | bytes 12582912 | tf_op jit(solution)/shard_map/dot_general | solution.py:301
  92.0 32.0 %shard_map.43 = f32[8,256]{1,0:T(8,128)} custom-call(f32[256,2048]{1,0:T(8,128)} %fusion.local_ref), custom_call_target="tpu_custom_call" | custom-call | tf_op jit(solution)/shard_map/pallas_call | solution.py:203
  124.1 1.3 %broadcast_multiply_fusion = f32[8,256]{1,0:T(8,128)} fusion(f32[8,256]{1,0:T(8,128)} %shard_map.43), kind=kLoop, calls=%fused_computation.3 | loop fusion | flops 2048 | bytes 16384 | tf_op jit(solution)/shard_map/mul | solution.py:305
Async XLA Ops:
  0.6 1.2 copy-start
  83.6 1.3 %copy-start.1 = (f32[2048,256]{1,0:T(8,128)}, f32[2048,256]{1,0:T(8,128)S(1)}, u32[]{:S(2)}) copy-start(f32[2048,256]{1,0:T(8,128)S(1)} %convolution_multiply_fusion) | copy-start | bytes 6291460

commit v11 on v10

--- a/solution.py
+++ b/solution.py
@@ -126,7 +126,7 @@
     return out
 
 
-def projection_kernel(n_rows, n_cols, local_ref, out_ref, from_core, by_chip, from_chip, part, from_row,
+def projection_kernel(n_rows, n_cols, factor, local_ref, out_ref, from_core, by_chip, from_chip, part, from_row,
                       send_a, arrive_a, send_b, arrive_b, send_c, arrive_c):
     me_r = lax.axis_index("rows")
     me_c = lax.axis_index("cols")
@@ -190,10 +190,10 @@
     along(n_rows, me_r, lambda r: copy(from_row.at[r], from_row.at[r], send_c.at[r], arrive_c.at[r],
                                        (r, me_c)).wait_recv())
     along(n_rows, me_r, lambda r: scatter(r).wait_send())
-    out_ref[...] = jnp.sum(from_row[...], axis=0)
-
-
-def reduce_projection(partial):
+    out_ref[...] = jnp.sum(from_row[...], axis=0) * factor
+
+
+def reduce_projection(partial, factor):
     n_rows = lax.axis_size("rows")
     n_cols = lax.axis_size("cols")
     rank, grid = partial.shape
@@ -201,7 +201,7 @@
     share = rank // n_rows
     n_chips = n_cols // 2
     return pl.pallas_call(
-        functools.partial(projection_kernel, n_rows, n_cols),
+        functools.partial(projection_kernel, n_rows, n_cols, factor),
         out_shape=jax.ShapeDtypeStruct((share, width), partial.dtype),
         in_specs=[pl.BlockSpec(memory_space=pltpu.VMEM)],
         out_specs=pl.BlockSpec(memory_space=pltpu.VMEM),
@@ -301,8 +301,7 @@
     partial = lax.dot_general(
         basis_half, snapshots, (((0,), (0,)), ((), ())), preferred_element_type=jnp.float32
     )
-    projected = reduce_projection(partial)
-    coeffs = projected * (1.0 / math.sqrt(total_rows))
+    coeffs = reduce_projection(partial, 1.0 / math.sqrt(total_rows))
     return (basis_full, coeffs)
 
 

time: 126 us -> 126 us (level)
  other arithmetic: 1.3 us -> 0 us
  local copies, waits for them, and re-layouts: 2.54 us -> 3.83 us
    mul x1 -> x0, other arithmetic: 1.3 us -> none  [body(): coeffs = projected * (1.0 / math.sqrt(total_rows))]
    unnamed x4 -> x5, local copies, waits for them, and re-layouts: 2.54 us -> 3.83 us
where the time goes in v11:
time: 126 us; the launch traced here: 125 us
  Pallas kernels  101 us (80%)
  matrix products  19.9 us (16%)
  local copies, waits for them, and re-layouts  3.83 us (3%)
    pallas_call x1, Pallas kernels, all_reduce(): pl.pallas_call(functools.partial(all_reduce_kernel, n_rows, n_cols), out_...  36.5 us
    pallas_call x1, Pallas kernels, lower_inverse(): pl.pallas_call(lower_inverse_kernel, out_shape=jax.ShapeDtypeStruct(gram....  32.4 us
    pallas_call x1, Pallas kernels, reduce_projection(): pl.pallas_call(functools.partial(projection_kernel, n_rows, n_cols, facto...  32 us
    dot_general x1, matrix products, body(): lax.dot_general(basis_half, snapshots, (((0,), (0,)), ((), ())), preferre...  7.13 us
    dot_general x1, matrix products, body(): sketch = jnp.dot(snapshots, test_matrix, preferred_element_type=jnp.float32)  5.73 us
    dot_general x1, matrix products, cross_product(): lax.dot_general(left, right, (((0,), (0,)), ((), ())), precision=lax.Prec...  4.19 us
    unnamed x5, local copies, waits for them, and re-layouts  3.83 us
    dot_general x1, matrix products, body(): lax.dot_general(sketch, inverse_low, (((1,), (1,)), ((), ())), precision=...  2.88 us

profile of v11, /device:TPU:1, one launch (start us, length us, event | category | flops | bytes accessed | tf_op | source)
XLA Modules:
  0.0 125.4 jit_solution(13449025007262116166)
XLA Ops:
  0.6 0.0 copy-start
  0.6 1.2 copy-done
  1.9 5.7 %fusion.2 = f32[2048,256]{1,0:T(8,128)S(1)} fusion(bf16[2048,2048]{1,0:T(8,128)(2,1)} %param.2, bf16[2048,256]{1,0:T(8,128)(2,1)S(1)} %copy-done), kind=kOutput, calls=%fused_computation.3 | convolution fusion | flops 2147483648 | bytes 11534336 | tf_op jit(solution)/shard_map/dot_general | solution.py:289
  7.6 4.2 %fusion.3 = f32[256,256]{1,0:T(8,128)} fusion(f32[2048,256]{1,0:T(8,128)S(1)} %fusion.2), kind=kOutput, calls=%fused_computation.4 | convolution fusion | flops 1610612736 | bytes 2359296 | tf_op jit(solution)/shard_map/dot_general | solution.py:13
  11.8 36.5 %shard_map.41.gram_ref = f32[256,256]{1,0:T(8,128)} custom-call(f32[8,32,256]{2,1,0:T(8,128)} %bitcast.8), custom_call_target="tpu_custom_call" | custom-call | tf_op jit(solution)/shard_map/pallas_call | solution.py:104
  48.3 32.4 %shard_map.42 = f32[256,256]{1,0:T(8,128)} custom-call(f32[256,256]{1,0:T(8,128)} %shard_map.41.gram_ref), custom_call_target="tpu_custom_call" | custom-call | tf_op jit(solution)/shard_map/pallas_call | solution.py:275
  80.7 2.9 %convolution_multiply_fusion = f32[2048,256]{1,0:T(8,128)S(1)} fusion(f32[2048,256]{1,0:T(8,128)S(1)} %fusion.2, f32[256,256]{1,0:T(8,128)} %shard_map.42), kind=kOutput, calls=%fused_computation | convolution fusion | flops 1611137024 | bytes 4456448 | tf_op jit(solution)/shard_map/dot_general | solution.py:293
  83.6 0.0 copy-start.1
  83.6 1.3 %copy-done.1 = f32[2048,256]{1,0:T(8,128)} copy-done((f32[2048,256]{1,0:T(8,128)}, f32[2048,256]{1,0:T(8,128)S(1)}, u32[]{:S(2)}) %copy-start.1) | copy-done | bytes 2097176
  84.9 7.1 %fusion.local_ref = f32[256,2048]{1,0:T(8,128)} fusion(bf16[2048,2048]{1,0:T(8,128)(2,1)} %param.2, f32[2048,256]{1,0:T(8,128)S(1)} %convolution_multiply_fusion), kind=kOutput, calls=%fused_computation.1 | convolution fusion | flops 2148007936 | bytes 12582912 | tf_op jit(solution)/shard_map/dot_general | solution.py:301
  92.0 32.0 %shard_map.43 = f32[8,256]{1,0:T(8,128)} custom-call(f32[256,2048]{1,0:T(8,128)} %fusion.local_ref), custom_call_target="tpu_custom_call" | custom-call | tf_op jit(solution)/shard_map/pallas_call | solution.py:203
  124.1 1.3 %copy.5 = f32[8,256]{1,0:T(8,128)} copy(f32[8,256]{1,0:T(8,128)} %shard_map.43) | data formatting | bytes 16384
Async XLA Ops:
  0.6 1.2 copy-start
  83.6 1.3 %copy-start.1 = (f32[2048,256]{1,0:T(8,128)}, f32[2048,256]{1,0:T(8,128)S(1)}, u32[]{:S(2)}) copy-start(f32[2048,256]{1,0:T(8,128)S(1)} %convolution_multiply_fusion) | copy-start | bytes 6291460

commit v12 on v10

--- a/solution.py
+++ b/solution.py
@@ -28,7 +28,7 @@
     return lax.all_to_all(chunks, axis, 0, 0, tiled=True).sum(0)
 
 
-def all_reduce_kernel(n_rows, n_cols, local_ref, out_ref, recv1, part, recv2, total, rows_in,
+def all_reduce_kernel(n_rows, n_cols, sketch_ref, out_ref, local_ref, recv1, part, recv2, total, rows_in,
                       send1, arrive1, send2, arrive2, send3, arrive3, send4, arrive4):
     me_r = lax.axis_index("rows")
     me_c = lax.axis_index("cols")
@@ -51,6 +51,10 @@
         barrier, inc=1, device_id=(me_r, c), device_id_type=pl.DeviceIdType.MESH))
     along(n_rows, me_r, lambda r: pl.semaphore_signal(
         barrier, inc=1, device_id=(r, me_c), device_id_type=pl.DeviceIdType.MESH))
+    gram = cross_product(sketch_ref[...], sketch_ref[...])
+    block = local_ref.shape[1]
+    for c in range(n_cols):
+        local_ref[c] = gram[c * block:(c + 1) * block]
     pl.semaphore_wait(barrier, n_cols + n_rows - 2)
 
     def scatter1(c):
@@ -96,9 +100,10 @@
     along(n_cols, me_c, lambda c: gather4(c).wait_send())
 
 
-def all_reduce(x):
+def all_reduce(sketch):
     n_rows = lax.axis_size("rows")
     n_cols = lax.axis_size("cols")
+    x = jax.ShapeDtypeStruct((sketch.shape[1], sketch.shape[1]), sketch.dtype)
     rows, width = x.shape
     block = rows // n_cols
     out = pl.pallas_call(
@@ -108,6 +113,7 @@
         out_specs=pl.BlockSpec(memory_space=pltpu.VMEM),
         scratch_shapes=[
             pltpu.VMEM((n_cols, block, width), x.dtype),
+            pltpu.VMEM((n_cols, block, width), x.dtype),
             pltpu.VMEM((n_rows, block // n_rows, width), x.dtype),
             pltpu.VMEM((n_rows, block // n_rows, width), x.dtype),
             pltpu.VMEM((block // n_rows, width), x.dtype),
@@ -122,7 +128,7 @@
             pltpu.SemaphoreType.DMA((n_cols,)),
         ],
         compiler_params=pltpu.CompilerParams(collective_id=0, has_side_effects=True),
-    )(x.reshape(n_cols, block, width))
+    )(sketch)
     return out
 
 
@@ -287,8 +293,7 @@
     rows_here = snapshots.shape[0]
     total_rows = rows_here * n_rows * n_cols
     sketch = jnp.dot(snapshots, test_matrix, preferred_element_type=jnp.float32)
-    gram_local = cross_product(sketch, sketch)
-    summed = all_reduce(gram_local)
+    summed = all_reduce(sketch)
     inverse_low = lower_inverse(summed)
     basis_full = lax.dot_general(
         sketch,

time: 126 us -> 124 us (0.984)
  matrix products: 19.9 us -> 18.3 us
  local copies, waits for them, and re-layouts: 2.54 us -> 1.23 us
    dot_general x1 -> x0, matrix products: 4.19 us -> none  [cross_product(): lax.dot_general(left, right, (((0,), (0,)), ((), ())), precision=lax.Prec...]
    dot_general x1, matrix products: 5.73 us -> 7.05 us  [body(): sketch = jnp.dot(snapshots, test_matrix, preferred_element_type=jnp.float32)]
    unnamed x4, local copies, waits for them, and re-layouts: 2.54 us -> 1.23 us
where the time goes in v12:
time: 124 us; the launch traced here: 123 us
  Pallas kernels  102 us (82%)
  matrix products  18.3 us (15%)
  other arithmetic  1.3 us (1%)
    pallas_call x1, Pallas kernels, all_reduce(): pl.pallas_call(functools.partial(all_reduce_kernel, n_rows, n_cols), out_...  37.1 us
    pallas_call x1, Pallas kernels, lower_inverse(): pl.pallas_call(lower_inverse_kernel, out_shape=jax.ShapeDtypeStruct(gram....  32.4 us
    pallas_call x1, Pallas kernels, reduce_projection(): pl.pallas_call(functools.partial(projection_kernel, n_rows, n_cols), out_...  32.2 us
    dot_general x1, matrix products, body(): lax.dot_general(basis_half, snapshots, (((0,), (0,)), ((), ())), preferre...  7.83 us
    dot_general x1, matrix products, body(): sketch = jnp.dot(snapshots, test_matrix, preferred_element_type=jnp.float32)  7.05 us
    dot_general x1, matrix products, body(): lax.dot_general(sketch, inverse_low, (((1,), (1,)), ((), ())), precision=...  3.43 us

profile of v12, /device:TPU:1, one launch (start us, length us, event | category | flops | bytes accessed | tf_op | source)
XLA Modules:
  0.0 123.2 jit_solution(3488528032870450619)
XLA Ops:
  0.6 0.0 copy-start
  0.6 1.2 copy-done
  1.9 7.0 %fusion.2.sketch_ref = f32[2048,256]{1,0:T(8,128)} fusion(bf16[2048,2048]{1,0:T(8,128)(2,1)} %param.2, bf16[2048,256]{1,0:T(8,128)(2,1)S(1)} %copy-done), kind=kOutput, calls=%fused_computation.4 | convolution fusion | flops 2147483648 | bytes 11534336 | tf_op jit(solution)/shard_map/dot_general | solution.py:295
  8.9 37.1 %shard_map.41.gram_ref = f32[256,256]{1,0:T(8,128)} custom-call(f32[2048,256]{1,0:T(8,128)} %fusion.2.sketch_ref), custom_call_target="tpu_custom_call" | custom-call | tf_op jit(solution)/shard_map/pallas_call | solution.py:109
  46.1 32.4 %shard_map.42 = f32[256,256]{1,0:T(8,128)} custom-call(f32[256,256]{1,0:T(8,128)} %shard_map.41.gram_ref), custom_call_target="tpu_custom_call" | custom-call | tf_op jit(solution)/shard_map/pallas_call | solution.py:281
  78.4 3.4 %convolution_multiply_fusion = f32[2048,256]{1,0:T(8,128)S(1)} fusion(f32[2048,256]{1,0:T(8,128)} %fusion.2.sketch_ref, f32[256,256]{1,0:T(8,128)} %shard_map.42), kind=kOutput, calls=%fused_computation | convolution fusion | flops 1611137024 | bytes 4456448 | tf_op jit(solution)/shard_map/dot_general | solution.py:298
  81.9 0.0 copy-start.1
  81.9 7.8 %fusion.local_ref = f32[256,2048]{1,0:T(8,128)} fusion(bf16[2048,2048]{1,0:T(8,128)(2,1)} %param.2, f32[2048,256]{1,0:T(8,128)S(1)} %convolution_multiply_fusion), kind=kOutput, calls=%fused_computation.1 | convolution fusion | flops 2148007936 | bytes 12582912 | tf_op jit(solution)/shard_map/dot_general | solution.py:306
  89.7 0.0 copy-done.1
  89.7 32.2 %shard_map.43 = f32[8,256]{1,0:T(8,128)} custom-call(f32[256,2048]{1,0:T(8,128)} %fusion.local_ref), custom_call_target="tpu_custom_call" | custom-call | tf_op jit(solution)/shard_map/pallas_call | solution.py:209
  121.9 1.3 %broadcast_multiply_fusion = f32[8,256]{1,0:T(8,128)} fusion(f32[8,256]{1,0:T(8,128)} %shard_map.43), kind=kLoop, calls=%fused_computation.3 | loop fusion | flops 2048 | bytes 16384 | tf_op jit(solution)/shard_map/mul | solution.py:310
Async XLA Ops:
  0.6 1.2 copy-start
  81.9 7.8 %copy-start.1 = (f32[2048,256]{1,0:T(8,128)}, f32[2048,256]{1,0:T(8,128)S(1)}, u32[]{:S(2)}) copy-start(f32[2048,256]{1,0:T(8,128)S(1)} %convolution_multiply_fusion) | copy-start | bytes 6291460
